TPU v7x, 32 devices: a whole 2x2x4 slice. The times are simulated.
32 devices in a mesh: ctx: 16 (over z, y, core), tp: 2 (over x).
Axes of the slice: x: 2, y: 2, z: 4, core: 2. Of those that a mesh axis runs over, the one named last changes fastest.
Arguments:
- activations: bfloat16 [2048, 4096], P(('ctx', 'tp')), may hold values from -24 to 24
- query_weight: bfloat16 [4096, 4096], P(None, 'tp'), may hold values from -0.09375 to 0.09375
- key_weight: bfloat16 [4096, 1024], P(None, 'tp'), may hold values from -0.09375 to 0.09375
- value_weight: bfloat16 [4096, 1024], P(None, 'tp'), may hold values from -0.09375 to 0.09375
Outputs:
- attended: bfloat16 [2048, 4096], P('ctx', 'tp')
All inputs are finite; a program needn't handle non-finite values.
Results may differ from a plain program's by a relative error of at most 0.012.
The roundings to bfloat16 on the way count: a program that leaves them out, or rounds other values in their place, can miss the bound.
Values may be sent and summed in bfloat16 or wider, within the bound.
No kernel may reach another device: no remote copies, remote signals or barrier semaphores. Data moves between devices by JAX's collectives and lax.ppermute only.
A program may use at most 128 MiB of HBM per device.

v0:
```python
import math

import jax
import jax.numpy as jnp
from jax import lax
from jax.sharding import PartitionSpec as P

HD = 128


THETA = 500000.0
NEGATIVE = -1e30


def rotate(heads_in, positions):
    width = heads_in.shape[-1]
    half_width = width // 2
    frequency = THETA ** (-(jnp.arange(half_width).astype(jnp.float32) * 2.0 / width))
    angles = positions[:, None] * frequency[None, :]
    cosine = jnp.cos(angles)[:, None, :]
    sine_table = jnp.sin(angles)[:, None, :]
    front_half = heads_in[..., :half_width]
    back_half = heads_in[..., half_width:]
    return jnp.concatenate(
        [
            front_half * cosine - back_half * sine_table,
            back_half * cosine + front_half * sine_table,
        ],
        axis=-1,
    )


def block_update(state, query_block, query_pos, key_block, value_block, key_pos):
    row_top, totals, accum = state
    scale = 1.0 / math.sqrt(query_block.shape[-1])
    scores = (
        lax.dot_general(
            query_block, key_block, (((1,), (1,)), ((), ())), preferred_element_type=jnp.float32
        )
        * scale
    )
    allowed = key_pos[None, :] <= query_pos[:, None]
    block_top = jnp.max(jnp.where(allowed, scores, NEGATIVE), axis=1)
    new_top = jnp.maximum(row_top, block_top)
    correction = jnp.exp(row_top - new_top)
    weights = jnp.where(allowed, jnp.exp(scores - new_top[:, None]), 0.0)
    totals = totals * correction + jnp.sum(weights, axis=1)
    accum = accum * correction[:, None] + jnp.dot(
        weights.astype(jnp.bfloat16), value_block, preferred_element_type=jnp.float32
    )
    return (new_top, totals, accum)


def attend(groups, keys, values):
    carry_start = []
    for query_rows, query_pos, kv_slot, query_step in groups:
        row_count = query_rows.shape[0]
        blocks_count = row_count // query_step
        carry_start.append(
            (
                jnp.full((blocks_count, query_step), NEGATIVE, jnp.float32),
                jnp.zeros((blocks_count, query_step), jnp.float32),
                jnp.zeros((blocks_count, query_step, HD), jnp.float32),
            )
        )
    carry = tuple(carry_start)
    key_piece = lax.all_gather(keys, "ctx", axis=0, tiled=True)
    value_piece = lax.all_gather(values, "ctx", axis=0, tiled=True)
    piece_rows = key_piece.shape[0]
    key_step = math.gcd(piece_rows, 512)
    updated = []
    for (query_rows, query_pos, kv_slot, query_step), fold_state in zip(groups, carry):
        key_chosen = lax.dynamic_index_in_dim(
            key_piece.reshape(piece_rows, -1, HD), kv_slot, 1, keepdims=False
        )
        value_chosen = lax.dynamic_index_in_dim(
            value_piece.reshape(piece_rows, -1, HD), kv_slot, 1, keepdims=False
        )
        key_blocks = key_chosen.reshape(piece_rows // key_step, key_step, HD)
        value_blocks = value_chosen.reshape(piece_rows // key_step, key_step, HD)
        block_starts = jnp.arange(piece_rows // key_step, dtype=jnp.int32) * key_step
        blocks_count = fold_state[0].shape[0]
        query_blocks = query_rows.reshape(blocks_count, query_step, HD)
        pos_blocks = query_pos.reshape(blocks_count, query_step)

        def per_query(items):
            query_block, pos_block, row_top, totals, accum = items
            last_pos = jnp.max(pos_block)

            def per_key(inner, key_items):
                key_block, value_block, key_start = key_items
                key_pos = key_start + jnp.arange(key_step, dtype=jnp.int32)
                result = lax.cond(
                    key_start <= last_pos,
                    lambda current: block_update(
                        current, query_block, pos_block, key_block, value_block, key_pos
                    ),
                    lambda current: current,
                    inner,
                )
                return (result, None)

            final, unused = lax.scan(
                per_key, (row_top, totals, accum), (key_blocks, value_blocks, block_starts)
            )
            return final

        updated.append(
            lax.map(
                per_query, (query_blocks, pos_blocks, fold_state[0], fold_state[1], fold_state[2])
            )
        )
    final_state = tuple(updated)
    results = []
    for state in final_state:
        outcome = state[2] / state[1][..., None]
        results.append(outcome.reshape(-1, HD))
    return results


def local(activations, query_weight, key_weight, value_weight):
    tensor_count = lax.axis_size("tp")
    context_index = lax.axis_index("ctx")
    local_rows = activations.shape[0] * tensor_count
    heads_here = query_weight.shape[1] // HD
    kv_here = key_weight.shape[1] // HD
    group = heads_here // kv_here
    query_width = heads_here * HD
    key_width = kv_here * HD
    gathered = lax.all_gather(activations, "tp", axis=0, tiled=True)
    projected = jnp.concatenate(
        [
            jnp.dot(gathered, query_weight, preferred_element_type=jnp.float32),
            jnp.dot(gathered, key_weight, preferred_element_type=jnp.float32),
            jnp.dot(gathered, value_weight, preferred_element_type=jnp.float32),
        ],
        axis=1,
    )
    token_pos = context_index * local_rows + jnp.arange(local_rows, dtype=jnp.int32)
    positions = token_pos.astype(jnp.float32)
    queries = rotate(
        projected[:, :query_width].reshape(local_rows, heads_here, HD), positions
    ).astype(jnp.bfloat16)
    keys = (
        rotate(
            projected[:, query_width : query_width + key_width].reshape(local_rows, kv_here, HD),
            positions,
        )
        .astype(jnp.bfloat16)
        .reshape(local_rows, key_width)
    )
    values = projected[:, query_width + key_width :].astype(jnp.bfloat16)
    groups = []
    for kv_slot in range(kv_here):
        chosen = queries[:, kv_slot * group : (kv_slot + 1) * group].reshape(local_rows * group, HD)
        groups.append(
            (chosen, jnp.repeat(token_pos, group), kv_slot, math.gcd(local_rows * group, 512))
        )
    results = attend(groups, keys, values)
    pieces = [outcome.astype(jnp.bfloat16).reshape(local_rows, group * HD) for outcome in results]
    return jnp.concatenate(pieces, axis=1)


def solution(mesh):
    in_specs = (P(("ctx", "tp"), None), P(None, "tp"), P(None, "tp"), P(None, "tp"))
    out_specs = P("ctx", "tp")
    return jax.shard_map(local, mesh=mesh, in_specs=in_specs, out_specs=out_specs, check_vma=False)
```

profile of v0, /device:TPU:25, one launch (start us, length us, event | category | flops | bytes accessed | tf_op | source)
XLA Modules:
  0.0 219.5 jit_solution(12466268835597819170)
XLA Ops:
  7.6 23.6 %all-gather.4.cloned.1.call-done = bf16[128,4096]{1,0:T(8,128)(2,1)} async-done(((bf16[64,4096]{1,0:T(8,128)(2,1)}), bf16[128,4096]{1,0:T(8,128)(2,1)}) %all-gather.4.cloned.1.call-update) | async-done | bytes 1048592 | tf_op jit(solution)/shard_map/all_gather | solution.py:130
  31.2 3.3 %fusion.78 = f32[128,512]{1,0:T(8,128)S(1)} fusion(bf16[128,4096]{1,0:T(8,128)(2,1)} %all-gather.4.cloned.1.call-done, bf16[4096,512]{1,0:T(8,128)(2,1)} %param.22), kind=kOutput, calls=%fused_computation.123 | convolution fusion | flops 536870912 | bytes 5505024 | tf_op jit(solution)/shard_map/dot_general | solution.py:134
  36.0 3.6 %convolution_convert_fusion = bf16[128,512]{1,0:T(8,128)(2,1)} fusion(bf16[128,4096]{1,0:T(8,128)(2,1)S(1)} %copy-done, bf16[4096,512]{1,0:T(8,128)(2,1)} %param.23), kind=kOutput, calls=%fused_computation.93 | convolution fusion | flops 536936448 | bytes 5373952 | tf_op jit(solution)/shard_map/dot_general | solution.py:135
  40.3 8.2 %convolution_bitcast_fusion = f32[16,8,16,128]{3,1,2,0:T(8,128)S(1)} fusion(bf16[128,4096]{1,0:T(8,128)(2,1)S(1)} %copy-done, bf16[4096,2048]{1,0:T(8,128)(2,1)} %param.21), kind=kOutput, calls=%fused_computation.92 | convolution fusion | flops 2147483648 | bytes 18874368 | tf_op jit(solution)/shard_map/dot_general | solution.py:133
  50.6 25.6 %all-gather.6.cloned.1.call-done = bf16[2048,512]{0,1:T(8,128)(2,1)} async-done(((bf16[128,512]{0,1:T(8,128)(2,1)}), bf16[2048,512]{0,1:T(8,128)(2,1)}) %all-gather.6.cloned.1.call-update) | async-done | bytes 2097168 | tf_op jit(solution)/shard_map/all_gather | solution.py:67
  76.1 2.7 %fusion.77 = (bf16[2048,1,128]{0,2,1:T(8,128)(2,1)S(1)}, bf16[2048,1,128]{0,2,1:T(8,128)(2,1)}, bf16[2048,1,128]{0,2,1:T(8,128)(2,1)}, bf16[2048,1,128]{0,2,1:T(8,128)(2,1)}) fusion(bf16[2048,4,128]{0,2,1:T(8,128)(2,1)} %bitcast.80), kind=kLoop, calls=%fused_computation.122 | loop fusion | bytes 4194304 | tf_op jit(solution)/shard_map/jit(dynamic_index_in_dim)/dynamic_slice | solution.py:73
  79.9 39.1 %all-gather.8.cloned.1.call-done = bf16[2048,512]{1,0:T(8,128)(2,1)} async-done(((bf16[128,512]{1,0:T(8,128)(2,1)}), bf16[2048,512]{1,0:T(8,128)(2,1)}) %all-gather.8.cloned.1.call-update) | async-done | bytes 2097168 | tf_op jit(solution)/shard_map/all_gather | solution.py:68
  121.5 4.0 %fusion.76 = (bf16[2048,1,128]{2,1,0:T(2,128)(2,1)S(1)}, bf16[2048,1,128]{2,1,0:T(2,128)(2,1)}, bf16[2048,1,128]{2,1,0:T(2,128)(2,1)}, bf16[2048,1,128]{2,1,0:T(2,128)(2,1)S(1)}) fusion(bf16[2048,4,128]{2,1,0:T(4,128)(2,1)S(1)} %reshape.177), kind=kLoop, calls=%fused_computation.121 | loop fusion | bytes 4194304 | tf_op jit(solution)/shard_map/jit(dynamic_index_in_dim)/dynamic_slice | solution.py:76
  126.5 22.5 %while.96 = (s32[]{:T(128)}, f32[512]{0:T(512)S(1)}, f32[512]{0:T(512)S(1)}, f32[512,128]{1,0:T(8,128)S(1)}, s32[4]{0:T(128)S(1)}, /*index=5*/s32[]{:T(128)}, bf...) while((s32[]{:T(128)}, f32[512]{0:T(512)S(1)}, ...), condition=%wide.region_6.7_spmd.clone, body=%wide.region_1.0_spmd.clone.sunk | while | flops 137496064 | bytes 4122387 | solution.py:103
  128.3 3.8 %conditional.12 = ((f32[512]{0:T(512)S(1)}, f32[512]{0:T(512)S(1)}, f32[512,128]{1,0:T(8,128)S(1)})) conditional(s32[]{:T(128)} %convert_element_type.119, (f32[512]{0:T(512)S(1)}, f32[512]{0:T(512)S(1)}, f32[512,128]{1,0:T(8,128)S(1)}) %tuple.163, (s32[]{:T(128)}, s32[512]{0:T(512)S(1)}, s32[128]{0:T(128)S(1)}, bf16[4,512,128]{2,1,0:T(8,128)(2,1)}, ...), branch_computations={%region_2.2_spmd, %region_3.5_spmd} | conditional | flops 137496064 | bytes 4120100 | solution.py:93
  133.9 3.8 %conditional.12 = ((f32[512]{0:T(512)S(1)}, f32[512]{0:T(512)S(1)}, f32[512,128]{1,0:T(8,128)S(1)})) conditional(s32[]{:T(128)} %convert_element_type.119, (f32[512]{0:T(512)S(1)}, f32[512]{0:T(512)S(1)}, f32[512,128]{1,0:T(8,128)S(1)}) %tuple.163, (s32[]{:T(128)}, s32[512]{0:T(512)S(1)}, s32[128]{0:T(128)S(1)}, bf16[4,512,128]{2,1,0:T(8,128)(2,1)}, ...), branch_computations={%region_2.2_spmd, %region_3.5_spmd} | conditional | flops 137496064 | bytes 4120100 | solution.py:93
  139.5 3.8 %conditional.12 = ((f32[512]{0:T(512)S(1)}, f32[512]{0:T(512)S(1)}, f32[512,128]{1,0:T(8,128)S(1)})) conditional(s32[]{:T(128)} %convert_element_type.119, (f32[512]{0:T(512)S(1)}, f32[512]{0:T(512)S(1)}, f32[512,128]{1,0:T(8,128)S(1)}) %tuple.163, (s32[]{:T(128)}, s32[512]{0:T(512)S(1)}, s32[128]{0:T(128)S(1)}, bf16[4,512,128]{2,1,0:T(8,128)(2,1)}, ...), branch_computations={%region_2.2_spmd, %region_3.5_spmd} | conditional | flops 137496064 | bytes 4120100 | solution.py:93
  145.2 3.8 %conditional.12 = ((f32[512]{0:T(512)S(1)}, f32[512]{0:T(512)S(1)}, f32[512,128]{1,0:T(8,128)S(1)})) conditional(s32[]{:T(128)} %convert_element_type.119, (f32[512]{0:T(512)S(1)}, f32[512]{0:T(512)S(1)}, f32[512,128]{1,0:T(8,128)S(1)}) %tuple.163, (s32[]{:T(128)}, s32[512]{0:T(512)S(1)}, s32[128]{0:T(128)S(1)}, bf16[4,512,128]{2,1,0:T(8,128)(2,1)}, ...), branch_computations={%region_2.2_spmd, %region_3.5_spmd} | conditional | flops 137496064 | bytes 4120100 | solution.py:93
  151.2 23.1 %while.97 = (s32[]{:T(128)}, f32[512]{0:T(512)S(1)}, f32[512]{0:T(512)S(1)}, f32[512,128]{1,0:T(8,128)S(1)}, s32[4]{0:T(128)S(1)}, /*index=5*/s32[]{:T(128)}, bf...) while((s32[]{:T(128)}, f32[512]{0:T(512)S(1)}, ...), condition=%wide.region_12.13_spmd.clone, body=%wide.region_7.12_spmd.clone.sunk | while | flops 137496064 | bytes 4122387 | solution.py:103
  153.1 3.9 %conditional.13 = ((f32[512]{0:T(512)S(1)}, f32[512]{0:T(512)S(1)}, f32[512,128]{1,0:T(8,128)S(1)})) conditional(s32[]{:T(128)} %convert_element_type.120, (f32[512]{0:T(512)S(1)}, f32[512]{0:T(512)S(1)}, f32[512,128]{1,0:T(8,128)S(1)}) %tuple.166, (s32[]{:T(128)}, s32[512]{0:T(512)S(1)}, s32[128]{0:T(128)S(1)}, bf16[4,512,128]{2,1,0:T(8,128)(2,1)}, ...), branch_computations={%region_8.8_spmd, %region_9.11_spmd} | conditional | flops 137496064 | bytes 4120100 | solution.py:93
  158.9 3.9 %conditional.13 = ((f32[512]{0:T(512)S(1)}, f32[512]{0:T(512)S(1)}, f32[512,128]{1,0:T(8,128)S(1)})) conditional(s32[]{:T(128)} %convert_element_type.120, (f32[512]{0:T(512)S(1)}, f32[512]{0:T(512)S(1)}, f32[512,128]{1,0:T(8,128)S(1)}) %tuple.166, (s32[]{:T(128)}, s32[512]{0:T(512)S(1)}, s32[128]{0:T(128)S(1)}, bf16[4,512,128]{2,1,0:T(8,128)(2,1)}, ...), branch_computations={%region_8.8_spmd, %region_9.11_spmd} | conditional | flops 137496064 | bytes 4120100 | solution.py:93
  164.7 3.9 %conditional.13 = ((f32[512]{0:T(512)S(1)}, f32[512]{0:T(512)S(1)}, f32[512,128]{1,0:T(8,128)S(1)})) conditional(s32[]{:T(128)} %convert_element_type.120, (f32[512]{0:T(512)S(1)}, f32[512]{0:T(512)S(1)}, f32[512,128]{1,0:T(8,128)S(1)}) %tuple.166, (s32[]{:T(128)}, s32[512]{0:T(512)S(1)}, s32[128]{0:T(128)S(1)}, bf16[4,512,128]{2,1,0:T(8,128)(2,1)}, ...), branch_computations={%region_8.8_spmd, %region_9.11_spmd} | conditional | flops 137496064 | bytes 4120100 | solution.py:93
  170.4 3.9 %conditional.13 = ((f32[512]{0:T(512)S(1)}, f32[512]{0:T(512)S(1)}, f32[512,128]{1,0:T(8,128)S(1)})) conditional(s32[]{:T(128)} %convert_element_type.120, (f32[512]{0:T(512)S(1)}, f32[512]{0:T(512)S(1)}, f32[512,128]{1,0:T(8,128)S(1)}) %tuple.166, (s32[]{:T(128)}, s32[512]{0:T(512)S(1)}, s32[128]{0:T(128)S(1)}, bf16[4,512,128]{2,1,0:T(8,128)(2,1)}, ...), branch_computations={%region_8.8_spmd, %region_9.11_spmd} | conditional | flops 137496064 | bytes 4120100 | solution.py:93
  175.7 19.9 %while.98 = (s32[]{:T(128)}, f32[512]{0:T(512)S(1)}, f32[512]{0:T(512)S(1)}, f32[512,128]{1,0:T(8,128)S(1)}, s32[4]{0:T(128)S(1)}, /*index=5*/s32[]{:T(128)}, bf...) while((s32[]{:T(128)}, f32[512]{0:T(512)S(1)}, ...), condition=%wide.region_18.19_spmd.clone, body=%wide.region_13.18_spmd.clone.sunk | while | flops 137496064 | bytes 4121879 | solution.py:103
  177.8 2.9 %conditional.14 = ((f32[512]{0:T(512)S(1)}, f32[512]{0:T(512)S(1)}, f32[512,128]{1,0:T(8,128)S(1)})) conditional(s32[]{:T(128)} %convert_element_type.121, (f32[512]{0:T(512)S(1)}, f32[512]{0:T(512)S(1)}, f32[512,128]{1,0:T(8,128)S(1)}) %tuple.169, (s32[]{:T(128)}, s32[512]{0:T(512)S(1)}, s32[128]{0:T(128)S(1)}, bf16[4,512,128]{2,1,0:T(8,128)(2,1)}, ...), branch_computations={%region_14.14_spmd, %region_15.17_spmd} | conditional | flops 137496064 | bytes 4119592 | solution.py:93
  182.7 2.9 %conditional.14 = ((f32[512]{0:T(512)S(1)}, f32[512]{0:T(512)S(1)}, f32[512,128]{1,0:T(8,128)S(1)})) conditional(s32[]{:T(128)} %convert_element_type.121, (f32[512]{0:T(512)S(1)}, f32[512]{0:T(512)S(1)}, f32[512,128]{1,0:T(8,128)S(1)}) %tuple.169, (s32[]{:T(128)}, s32[512]{0:T(512)S(1)}, s32[128]{0:T(128)S(1)}, bf16[4,512,128]{2,1,0:T(8,128)(2,1)}, ...), branch_computations={%region_14.14_spmd, %region_15.17_spmd} | conditional | flops 137496064 | bytes 4119592 | solution.py:93
  187.7 2.9 %conditional.14 = ((f32[512]{0:T(512)S(1)}, f32[512]{0:T(512)S(1)}, f32[512,128]{1,0:T(8,128)S(1)})) conditional(s32[]{:T(128)} %convert_element_type.121, (f32[512]{0:T(512)S(1)}, f32[512]{0:T(512)S(1)}, f32[512,128]{1,0:T(8,128)S(1)}) %tuple.169, (s32[]{:T(128)}, s32[512]{0:T(512)S(1)}, s32[128]{0:T(128)S(1)}, bf16[4,512,128]{2,1,0:T(8,128)(2,1)}, ...), branch_computations={%region_14.14_spmd, %region_15.17_spmd} | conditional | flops 137496064 | bytes 4119592 | solution.py:93
  192.7 2.9 %conditional.14 = ((f32[512]{0:T(512)S(1)}, f32[512]{0:T(512)S(1)}, f32[512,128]{1,0:T(8,128)S(1)})) conditional(s32[]{:T(128)} %convert_element_type.121, (f32[512]{0:T(512)S(1)}, f32[512]{0:T(512)S(1)}, f32[512,128]{1,0:T(8,128)S(1)}) %tuple.169, (s32[]{:T(128)}, s32[512]{0:T(512)S(1)}, s32[128]{0:T(128)S(1)}, bf16[4,512,128]{2,1,0:T(8,128)(2,1)}, ...), branch_computations={%region_14.14_spmd, %region_15.17_spmd} | conditional | flops 137496064 | bytes 4119592 | solution.py:93
  196.3 15.6 %while.99 = (s32[]{:T(128)}, f32[512]{0:T(512)S(1)}, f32[512]{0:T(512)S(1)}, f32[512,128]{1,0:T(8,128)S(1)}, s32[4]{0:T(128)S(1)}, /*index=5*/s32[]{:T(128)}, bf...) while((s32[]{:T(128)}, f32[512]{0:T(512)S(1)}, ...), condition=%wide.region_24.25_spmd.clone, body=%wide.region_19.24_spmd.clone.sunk | while | flops 137496064 | bytes 4121371 | solution.py:103
  (240 shorter events, 82.3 us)
Async XLA Ops:
  6.5 24.7 %all-gather.4.cloned.1.call-start = ((), (), s32[]{:S(2)}) async-start(), calls=%async_computation | async-start | bytes 1572864 | tf_op jit(solution)/shard_map/all_gather | solution.py:130
  7.3 68.9 %all-gather.6.cloned.1.call-start = ((), (), s32[]{:S(2)}) async-start(), calls=%async_computation.1 | async-start | bytes 2228224 | tf_op jit(solution)/shard_map/all_gather | solution.py:67
  31.2 4.8 %copy-start = (bf16[128,4096]{1,0:T(8,128)(2,1)S(1)}, bf16[128,4096]{1,0:T(8,128)(2,1)}, u32[]{:S(2)}) copy-start(bf16[128,4096]{1,0:T(8,128)(2,1)} %all-gather.4.cloned.1.call-done) | copy-start | bytes 3145732
  35.9 83.1 %all-gather.8.cloned.1.call-start = ((), (), s32[]{:S(2)}) async-start(), calls=%async_computation.2 | async-start | bytes 2228224 | tf_op jit(solution)/shard_map/all_gather | solution.py:68
  126.5 22.7 %copy-start.5 = (bf16[2048,1,128]{0,2,1:T(8,128)(2,1)S(1)}, bf16[2048,1,128]{0,2,1:T(8,128)(2,1)}, u32[]{:S(2)}) copy-start(bf16[2048,1,128]{0,2,1:T(8,128)(2,1)} %get-tuple-element.984) | copy-start | bytes 1572868
  126.5 23.7 %copy-start.2 = (bf16[2048,1,128]{2,1,0:T(2,128)(2,1)S(1)}, bf16[2048,1,128]{2,1,0:T(2,128)(2,1)}, u32[]{:S(2)}) copy-start(bf16[2048,1,128]{2,1,0:T(2,128)(2,1)} %get-tuple-element.979) | copy-start | bytes 1572868
  151.2 23.4 %copy-start.4 = (bf16[2048,1,128]{0,2,1:T(8,128)(2,1)S(1)}, bf16[2048,1,128]{0,2,1:T(8,128)(2,1)}, u32[]{:S(2)}) copy-start(bf16[2048,1,128]{0,2,1:T(8,128)(2,1)} %get-tuple-element.983) | copy-start | bytes 1572868
  151.2 24.4 %copy-start.1 = (bf16[2048,1,128]{2,1,0:T(2,128)(2,1)S(1)}, bf16[2048,1,128]{2,1,0:T(2,128)(2,1)}, u32[]{:S(2)}) copy-start(bf16[2048,1,128]{2,1,0:T(2,128)(2,1)} %get-tuple-element.978) | copy-start | bytes 1572868
  175.7 20.1 %copy-start.3 = (bf16[2048,1,128]{0,2,1:T(8,128)(2,1)S(1)}, bf16[2048,1,128]{0,2,1:T(8,128)(2,1)}, u32[]{:S(2)}) copy-start(bf16[2048,1,128]{0,2,1:T(8,128)(2,1)} %get-tuple-element.982) | copy-start | bytes 1572868
Sparse Core Ops, SparseCore 0:
  8.9 22.2 all-gather.3
  36.0 40.0 all-gather.5
  78.3 40.6 all-gather.7
where the time goes:
time: 221 us; the launch traced here: 219 us
  waiting for transfers between devices  89 us (40%)
  matrix products  47.3 us (21%)
  local copies, waits for them, and re-layouts  28.9 us (13%)
  loops' own time  21.6 us (10%)
  other arithmetic  19.1 us (9%)
  between operations  13.5 us (6%)
    all_gather x1, waiting for transfers between devices, attend(): value_piece = lax.all_gather(values, 'ctx', axis=0, tiled=True)  39.1 us
    all_gather x1, waiting for transfers between devices, attend(): key_piece = lax.all_gather(keys, 'ctx', axis=0, tiled=True)  25.6 us
    all_gather x1, waiting for transfers between devices, local(): gathered = lax.all_gather(activations, 'tp', axis=0, tiled=True)  23.6 us
    another operation x4, loops' own time, per_query(): lax.scan(per_key, (row_top, totals, accum), (key_blocks, value_blocks, bl...  20.8 us
    dot_general x16, matrix products, block_update(): lax.dot_general(query_block, key_block, (((1,), (1,)), ((), ())), preferr...  16.5 us
    dot_general x16, matrix products, block_update(): jnp.dot(weights.astype(jnp.bfloat16), value_block, preferred_element_type...  15.7 us
    add x16, other arithmetic, per_key(): key_pos = key_start + jnp.arange(key_step, dtype=jnp.int32)  10.2 us
    dynamic_slice x16, local copies, waits for them, and re-layouts, per_query(): lax.scan(per_key, (row_top, totals, accum), (key_blocks, value_blocks, bl...  9.76 us
  transfers between devices with their start and end apart: 3, of which 3 were waited for; matrix products, arithmetic and copies ran while one was open for 8% of the time, Pallas kernels for 0%

commit v1 on v0

v1 whole, which is shorter than its diff:
```python
import functools
import math

import jax
import jax.numpy as jnp
from jax import lax
from jax.experimental import pallas as pl
from jax.experimental.pallas import tpu as pltpu
from jax.sharding import PartitionSpec as P

HD = 128
THETA = 500000.0
NEGATIVE = -1e30
VMEM = pl.BlockSpec(memory_space=pltpu.VMEM)
LIMIT = 48 * 1024 * 1024


def tables(positions):
    frequency = THETA ** (-(jnp.arange(HD // 2).astype(jnp.float32) * 2.0 / HD))
    angles = positions.astype(jnp.float32)[:, None] * frequency[None, :]
    cosine, sine = jnp.cos(angles), jnp.sin(angles)
    return jnp.concatenate([cosine, cosine], axis=1), jnp.concatenate([-sine, sine], axis=1)


def turn(head, cosine, sine):
    return head * cosine + pltpu.roll(head, HD // 2, 1) * sine


def kv_kernel(parts, kv_heads, which_ref, *refs):
    rows_in = refs[:parts]
    key_w, value_w, cosine, sine, out_ref, total = refs[parts:]
    step = pl.program_id(0)
    depth = key_w.shape[0]
    rows = jnp.concatenate(
        [r[:, pl.ds(pl.multiple_of(step * depth, depth), depth)] for r in rows_in], axis=0
    )
    width = kv_heads * HD
    keys = jnp.dot(rows, key_w[...], preferred_element_type=jnp.float32)
    values = jnp.dot(rows, value_w[...], preferred_element_type=jnp.float32)

    @pl.when(step == 0)
    def _():
        total[:, :width] = keys
        total[:, width:] = values

    @pl.when(step > 0)
    def _():
        total[:, :width] += keys
        total[:, width:] += values

    @pl.when(step == pl.num_programs(0) - 1)
    def _():
        for h in range(kv_heads):
            cut = slice(h * HD, (h + 1) * HD)
            out_ref[:, cut] = turn(total[:, cut], cosine[...], sine[...]).astype(jnp.bfloat16)
        out_ref[:, width:] = total[:, width:].astype(jnp.bfloat16)


def project_kv(which, blocks, key_weight, value_weight, cosine, sine, kv_heads):
    rows = sum(b.shape[0] for b in blocks)
    model = key_weight.shape[0]
    width = kv_heads * HD
    depth = math.gcd(model, 1024)
    whole = lambda a: pl.BlockSpec(a.shape, lambda k, w: (0, 0))
    weight = pl.BlockSpec((depth, width), lambda k, w: (k, w[0]))
    return pl.pallas_call(
        functools.partial(kv_kernel, len(blocks), kv_heads),
        out_shape=jax.ShapeDtypeStruct((rows, 2 * width), jnp.bfloat16),
        grid_spec=pltpu.PrefetchScalarGridSpec(
            num_scalar_prefetch=1,
            grid=(model // depth,),
            in_specs=[whole(b) for b in blocks] + [weight, weight, whole(cosine), whole(sine)],
            out_specs=pl.BlockSpec((rows, 2 * width), lambda k, w: (0, 0)),
            scratch_shapes=[pltpu.VMEM((rows, 2 * width), jnp.float32)],
        ),
        compiler_params=pltpu.CompilerParams(vmem_limit_bytes=LIMIT),
        cost_estimate=pl.CostEstimate(
            flops=4 * rows * model * width, bytes_accessed=4 * model * width, transcendentals=0
        ),
    )(which, *blocks, key_weight, value_weight, cosine, sine)


def query_kernel(parts, which_ref, *refs):
    rows_in = refs[:parts]
    weight, cosine, sine, out_ref, gathered = refs[parts:]

    @pl.when(pl.program_id(0) == 0)
    def _():
        at = 0
        for r in rows_in:
            gathered[at : at + r.shape[0]] = r[...]
            at += r.shape[0]

    product = jnp.dot(gathered[...], weight[...], preferred_element_type=jnp.float32)
    for h in range(weight.shape[1] // HD):
        head = product[:, h * HD : (h + 1) * HD]
        out_ref[h] = turn(head, cosine[...], sine[...]).astype(jnp.bfloat16)


def project_q(which, blocks, query_weight, cosine, sine, heads):
    rows = sum(b.shape[0] for b in blocks)
    model = query_weight.shape[0]
    per_step = math.gcd(heads, 2)
    steps = heads // per_step
    whole = lambda a: pl.BlockSpec(a.shape, lambda k, w: (0, 0))
    return pl.pallas_call(
        functools.partial(query_kernel, len(blocks)),
        out_shape=jax.ShapeDtypeStruct((heads, rows, HD), jnp.bfloat16),
        grid_spec=pltpu.PrefetchScalarGridSpec(
            num_scalar_prefetch=1,
            grid=(steps,),
            in_specs=[whole(b) for b in blocks]
            + [
                pl.BlockSpec((model, per_step * HD), lambda n, w: (0, w[0] * steps + n)),
                whole(cosine),
                whole(sine),
            ],
            out_specs=pl.BlockSpec((per_step, rows, HD), lambda n, w: (n, 0, 0)),
            scratch_shapes=[pltpu.VMEM((rows, model), jnp.bfloat16)],
        ),
        compiler_params=pltpu.CompilerParams(vmem_limit_bytes=LIMIT),
        cost_estimate=pl.CostEstimate(
            flops=2 * rows * model * heads * HD, bytes_accessed=2 * model * heads * HD, transcendentals=0
        ),
    )(which, *blocks, query_weight, cosine, sine)


def attend_kernel(own_count, far_count, kv_heads, seen_ref, *refs):
    query_ref, query_pos, key_pos = refs[:3]
    own = refs[3 : 3 + own_count]
    far = refs[3 + own_count : 3 + own_count + far_count]
    out_ref = refs[3 + own_count + far_count]
    heads, rows, _ = query_ref.shape
    group = heads // kv_heads
    factor = math.log2(math.e) / math.sqrt(HD)
    allowed = key_pos[...] <= query_pos[...]
    hidden = [jnp.where(seen_ref[i] > 0, 0.0, -NEGATIVE) for i in range(far_count)]

    for kv_head in range(kv_heads):
        key_cut = slice(kv_head * HD, (kv_head + 1) * HD)
        value_cut = slice((kv_heads + kv_head) * HD, (kv_heads + kv_head + 1) * HD)

        @pl.loop(0, group)
        def _(member):
            head = kv_head * group + member
            query = query_ref[head]

            def score(block):
                return lax.dot_general(
                    query, block, (((1,), (1,)), ((), ())), preferred_element_type=jnp.float32
                )

            near = jnp.concatenate([score(r[:, key_cut]) for r in own], axis=1)
            near = jnp.where(allowed, near, NEGATIVE)
            top = jnp.max(near, axis=1, keepdims=True)
            distant = []
            for i, r in enumerate(far):
                scores = score(r[:, key_cut])
                distant.append(scores)
                top = jnp.maximum(top, jnp.max(scores, axis=1, keepdims=True) - hidden[i])
            limit = top * factor
            weights = jnp.exp2(near * factor - limit)
            total = jnp.sum(weights, axis=1, keepdims=True)
            weights = weights.astype(jnp.bfloat16)
            result = None
            at = 0
            for r in own:
                count = r.shape[0]
                term = jnp.dot(
                    weights[:, at : at + count], r[:, value_cut], preferred_element_type=jnp.float32
                )
                result = term if result is None else result + term
                at += count
            for i, r in enumerate(far):
                weights = jnp.exp2(distant[i] * factor - (limit + hidden[i]))
                total = total + jnp.sum(weights, axis=1, keepdims=True)
                result = result + jnp.dot(
                    weights.astype(jnp.bfloat16), r[:, value_cut], preferred_element_type=jnp.float32
                )
            out_ref[head] = (result / total).astype(jnp.bfloat16)


def attend(seen, queries, query_pos, key_pos, own, far, kv_heads):
    heads, rows, _ = queries.shape
    keys = sum(r.shape[0] for r in own) + sum(r.shape[0] for r in far)
    return pl.pallas_call(
        functools.partial(attend_kernel, len(own), len(far), kv_heads),
        out_shape=jax.ShapeDtypeStruct((heads, rows, HD), jnp.bfloat16),
        in_specs=[pl.BlockSpec(memory_space=pltpu.SMEM)] + [VMEM] * (3 + len(own) + len(far)),
        out_specs=VMEM,
        compiler_params=pltpu.CompilerParams(vmem_limit_bytes=LIMIT),
        cost_estimate=pl.CostEstimate(
            flops=4 * heads * rows * keys * HD,
            bytes_accessed=heads * rows * HD * 4,
            transcendentals=heads * rows * keys,
        ),
    )(seen, queries, query_pos, key_pos, *own, *far)


def local(activations, query_weight, key_weight, value_weight):
    tensor_count, context_count = lax.axis_size("tp"), lax.axis_size("ctx")
    tensor_index, context_index = lax.axis_index("tp"), lax.axis_index("ctx")
    rows_here = activations.shape[0]
    local_rows = rows_here * tensor_count
    heads_here = query_weight.shape[1] // HD
    kv_here = key_weight.shape[1] // HD
    pair = 2 if context_count % 2 == 0 and kv_here % 2 == 0 else 1
    kv_heads, heads = kv_here // pair, heads_here // pair
    places = context_count // pair
    inner = 2 ** (int(math.log2(places)) // 2) if places & (places - 1) == 0 else 1
    outer = places // inner
    half = context_index % pair
    place = context_index // pair
    far_out, far_in = place // inner, place % inner
    which = half.astype(jnp.int32)[None]

    def swap(block):
        return lax.ppermute(block, "ctx", [(i, i ^ 1) for i in range(context_count)])

    def device(o, i, c):
        return (o * inner + i) * pair + c

    blocks = [activations]
    owners = [tensor_index]
    for shift in range(1, tensor_count):
        blocks.append(
            lax.ppermute(activations, "tp", [(i, (i + shift) % tensor_count) for i in range(tensor_count)])
        )
        owners.append((tensor_index - shift) % tensor_count)
    held, starts = [], []
    for block, owner in zip(blocks, owners):
        for c in range(pair):
            held.append(block if c == 0 else swap(block))
            starts.append((place * pair + (half + c) % pair) * local_rows + owner * rows_here)
    positions = jnp.concatenate([s + jnp.arange(rows_here, dtype=jnp.int32) for s in starts])
    cosine, sine = tables(positions)

    own, far, seen = [], [], []
    piece = project_kv(which, held, key_weight, value_weight, cosine, sine, kv_heads)
    own.append(piece)
    columns = [piece]
    for hop in range(1, outer):
        links = [
            (device(o, i, c), device(o + hop, i, c))
            for o in range(outer - hop)
            for i in range(inner)
            for c in range(pair)
        ]
        columns.append(lax.ppermute(piece, "ctx", links))
        far.append(columns[-1])
        seen.append(far_out >= hop)
    for hop, column in enumerate(columns):
        for turn_by in range(1, inner):
            links = [
                (device(o, i, c), device(o, (i + turn_by) % inner, c))
                for o in range(hop, outer)
                for i in range(inner)
                for c in range(pair)
                if hop > 0 or i + turn_by < inner
            ]
            far.append(lax.ppermute(column, "ctx", links))
            seen.append((far_out >= hop) if hop > 0 else (far_in >= turn_by))
    queries = project_q(which, held, query_weight, cosine, sine, heads)
    seen = jnp.stack([s.astype(jnp.int32) for s in seen]) if seen else jnp.zeros((1,), jnp.int32)
    result = attend(seen, queries, positions[:, None], positions[None, :], own, far, kv_heads)

    result = result.reshape(heads, tensor_count, pair, rows_here, HD)
    result = jnp.transpose(result, (2, 1, 3, 0, 4))
    shift = jnp.stack(owners)
    result = jnp.zeros_like(result).at[:, shift].set(result) if tensor_count > 2 else (
        jnp.where(tensor_index == 0, result, result[:, ::-1]) if tensor_count == 2 else result
    )
    result = result.reshape(pair, local_rows, heads * HD)
    if pair == 1:
        return result[0]
    theirs = swap(result[1])
    first = jnp.where(half == 0, result[0], theirs)
    second = jnp.where(half == 0, theirs, result[0])
    return jnp.concatenate([first, second], axis=1)


def solution(mesh):
    in_specs = (P(("ctx", "tp"), None), P(None, "tp"), P(None, "tp"), P(None, "tp"))
    return jax.shard_map(local, mesh=mesh, in_specs=in_specs, out_specs=P("ctx", "tp"), check_vma=False)
```

time: 221 us -> 73.5 us (0.33)
  waiting for transfers between devices: 89 us -> 28.2 us
  matrix products: 47.3 us -> 0 us
  local copies, waits for them, and re-layouts: 28.9 us -> 1.72 us
  loops' own time: 21.6 us -> 0 us
  starting transfers between devices: 0.08 us -> 21.3 us
  Pallas kernels: 0 us -> 19.6 us
  other arithmetic: 19.1 us -> 1.85 us
  between operations: 13.5 us -> 0.23 us
    all_gather x3 -> x0, waiting for transfers between devices: 88.2 us -> none  [the longest x1 39.1 us: attend(): value_piece = lax.all_gather(values, 'ctx', axis=0, tiled=True)]
    dot_general x35 -> x0, matrix products: 47.3 us -> none  [the longest x16 16.5 us: block_update(): lax.dot_general(query_block, key_block, (((1,), (1,)), ((), ())), preferr...]
    ppermute x0 -> x11, waiting for transfers between devices: none -> 28.2 us  [the longest x3 12.3 us: local(): columns.append(lax.ppermute(piece, 'ctx', links))]
    another operation x20 -> x0, loops' own time: 21.6 us -> none  [the longest x4 20.8 us: per_query(): lax.scan(per_key, (row_top, totals, accum), (key_blocks, value_blocks, bl...]
    ppermute x0 -> x11, starting transfers between devices: none -> 21.3 us  [the longest x4 12.3 us: local(): far.append(lax.ppermute(column, 'ctx', links))]
    pallas_call x0 -> x3, Pallas kernels: none -> 19.6 us  [the longest x1 9.6 us: attend(): pl.pallas_call(functools.partial(attend_kernel, len(own), len(far), kv_he...]
    dynamic_slice x18 -> x0, local copies, waits for them, and re-layouts: 16.5 us -> none  [the longest x16 9.76 us: per_query(): lax.scan(per_key, (row_top, totals, accum), (key_blocks, value_blocks, bl...]
    add x33 -> x2, other arithmetic: 10.5 us -> 0.01 us  [local(): s + jnp.arange(rows_here, dtype=jnp.int32)]
  transfers between devices with their start and end apart: 3 -> 11, of which waited for: 3 -> 6; matrix products, arithmetic and copies ran while one was open for 8% -> 2% of each run, Pallas kernels for 0% -> 8%
where the time goes in v1:
time: 73.5 us; the launch traced here: 73 us
  waiting for transfers between devices  28.2 us (38%)
  starting transfers between devices  21.3 us (29%)
  Pallas kernels  19.6 us (27%)
  other arithmetic  1.85 us (3%)
  local copies, waits for them, and re-layouts  1.72 us (2%)
    ppermute x3, waiting for transfers between devices, local(): columns.append(lax.ppermute(piece, 'ctx', links))  12.3 us
    ppermute x4, starting transfers between devices, local(): far.append(lax.ppermute(column, 'ctx', links))  12.3 us
    ppermute x1, waiting for transfers between devices, local(): lax.ppermute(activations, 'tp', [(i, (i + shift) % tensor_count) for i in...  10.7 us
    pallas_call x1, Pallas kernels, attend(): pl.pallas_call(functools.partial(attend_kernel, len(own), len(far), kv_he...  9.6 us
    pallas_call x1, Pallas kernels, project_q(): pl.pallas_call(functools.partial(query_kernel, len(blocks)), out_shape=ja...  5.87 us
    pallas_call x1, Pallas kernels, project_kv(): pl.pallas_call(functools.partial(kv_kernel, len(blocks), kv_heads), out_s...  4.18 us
    ppermute x3, starting transfers between devices, swap(): lax.ppermute(block, 'ctx', [(i, i ^ 1) for i in range(context_count)])  3.98 us
    ppermute x3, starting transfers between devices, local(): columns.append(lax.ppermute(piece, 'ctx', links))  3.88 us
  transfers between devices with their start and end apart: 11, of which 6 were waited for; matrix products, arithmetic and copies ran while one was open for 2% of the time, Pallas kernels for 8%

profile of v1, /device:TPU:25, one launch (start us, length us, event | category | flops | bytes accessed | tf_op | source)
XLA Modules:
  0.0 73.0 jit_solution(277279030481692653)
XLA Ops:
  0.0 1.2 %collective-permute-start.1 = (bf16[64,4096]{1,0:T(8,128)(2,1)}, bf16[64,4096]{1,0:T(8,128)(2,1)S(1)}, u32[]{:S(2)}, u32[]{:S(2)}) collective-permute-start(bf16[64,4096]{1,0:T(8,128)(2,1)} %refs_0_.3), channel_id=1, source_target_pairs={{0,1},{1,0},{2,3},{3,2},{4,5},{5,4},{6,7},{7,6},{8,9},{9,8},{10,11... | collective-permute-start | bytes 1572872 | tf_op jit(solution)/shard_map/ppermute | solution.py:227
  1.2 1.0 %collective-permute-start = (bf16[64,4096]{1,0:T(8,128)(2,1)}, bf16[64,4096]{1,0:T(8,128)(2,1)S(1)}, u32[]{:S(2)}, u32[]{:S(2)}) collective-permute-start(bf16[64,4096]{1,0:T(8,128)(2,1)} %refs_0_.3), channel_id=1, source_target_pairs={{0,2},{2,0},{4,6},{6,4},{8,10},{10,8},{12,14},{14,12},{16,18},{18,... | collective-permute-start | bytes 1572872 | tf_op jit(solution)/shard_map/ppermute | solution.py:218
  2.3 10.7 %collective-permute-done.1.refs_2_ = bf16[64,4096]{1,0:T(8,128)(2,1)S(1)} collective-permute-done((bf16[64,4096]{1,0:T(8,128)(2,1)}, bf16[64,4096]{1,0:T(8,128)(2,1)S(1)}, u32[]{:S(2)}, u32[]{:S(2)}) %collective-permute-start.1) | collective-permute-done | bytes 524320 | tf_op jit(solution)/shard_map/ppermute | solution.py:227
  13.0 1.5 %collective-permute-start.2 = (bf16[64,4096]{1,0:T(8,128)(2,1)S(1)}, bf16[64,4096]{1,0:T(8,128)(2,1)S(1)}, u32[]{:S(2)}, u32[]{:S(2)}) collective-permute-start(bf16[64,4096]{1,0:T(8,128)(2,1)S(1)} %collective-permute-done.1.refs_2_), channel_id=1, source_target_pairs={{0,2},{2,0},{4,6},{6,4},{8,10},{10,8},{12,14},{14,12},{16,18},{18,... | collective-permute-start | bytes 1572872 | tf_op jit(solution)/shard_map/ppermute | solution.py:218
  14.6 0.5 fusion
  15.3 0.8 %collective-permute-done.2.refs_3_ = bf16[64,4096]{1,0:T(8,128)(2,1)S(1)} collective-permute-done((bf16[64,4096]{1,0:T(8,128)(2,1)S(1)}, bf16[64,4096]{1,0:T(8,128)(2,1)S(1)}, u32[]{:S(2)}, u32[]{:S(2)}) %collective-permute-start.2) | collective-permute-done | bytes 524320 | tf_op jit(solution)/shard_map/ppermute | solution.py:218
  16.1 1.0 %copy-done = bf16[64,4096]{1,0:T(8,128)(2,1)S(1)} copy-done((bf16[64,4096]{1,0:T(8,128)(2,1)S(1)}, bf16[64,4096]{1,0:T(8,128)(2,1)}, u32[]{:S(2)}) %copy-start) | copy-done | bytes 524312
  17.1 4.2 %shard_map.47.refs_3_ = bf16[256,512]{1,0:T(8,128)(2,1)S(1)} custom-call(s32[1]{0:T(128)} %bitcast.4.which_ref, bf16[64,4096]{1,0:T(8,128)(2,1)S(1)} %copy-done, bf16[64,4096]{1,0:T(8,128)(2,1)S(1)} %collective-permute-done.refs_1_, bf16[64,4096]{1,0:T(8,128)(2,1)S(1)} %collective-permute-done.1.refs_2_, ...), custom_call_target="tpu_custom_call" | custom-call | flops 1073741824 | bytes 4194304 | tf_op jit(solution)/shard_map/pallas_call | solution.py:66
  21.3 1.3 %collective-permute-start.5 = (bf16[256,512]{1,0:T(8,128)(2,1)S(1)}, bf16[256,512]{1,0:T(8,128)(2,1)S(1)}, u32[]{:S(2)}, u32[]{:S(2)}) collective-permute-start(bf16[256,512]{1,0:T(8,128)(2,1)S(1)} %shard_map.47.refs_3_), channel_id=1, source_target_pairs={{0,24},{2,26},{4,28},{6,30},{1,25},{3,27},{5,29},{7,31}} | collective-permute-start | bytes 786440 | tf_op jit(solution)/shard_map/ppermute | solution.py:249
  22.6 1.3 %collective-permute-start.4 = (bf16[256,512]{1,0:T(8,128)(2,1)S(1)}, bf16[256,512]{1,0:T(8,128)(2,1)S(1)}, u32[]{:S(2)}, u32[]{:S(2)}) collective-permute-start(bf16[256,512]{1,0:T(8,128)(2,1)S(1)} %shard_map.47.refs_3_), channel_id=1, source_target_pairs={{0,16},{2,18},{4,20},{6,22},{8,24},{10,26},{12,28},{14,30},{1,17},... | collective-permute-start | bytes 786440 | tf_op jit(solution)/shard_map/ppermute | solution.py:249
  23.9 1.3 %collective-permute-start.3 = (bf16[256,512]{1,0:T(8,128)(2,1)S(1)}, bf16[256,512]{1,0:T(8,128)(2,1)S(1)}, u32[]{:S(2)}, u32[]{:S(2)}) collective-permute-start(bf16[256,512]{1,0:T(8,128)(2,1)S(1)} %shard_map.47.refs_3_), channel_id=1, source_target_pairs={{0,8},{2,10},{4,12},{6,14},{8,16},{10,18},{12,20},{14,22},{16,24},... | collective-permute-start | bytes 786440 | tf_op jit(solution)/shard_map/ppermute | solution.py:249
  25.2 3.9 %collective-permute-start.6 = (bf16[256,512]{1,0:T(8,128)(2,1)S(1)}, bf16[256,512]{1,0:T(8,128)(2,1)}, u32[]{:S(2)}, u32[]{:S(2)}) collective-permute-start(bf16[256,512]{1,0:T(8,128)(2,1)S(1)} %shard_map.47.refs_3_), channel_id=1, source_target_pairs={{0,4},{2,6},{8,12},{10,14},{16,20},{18,22},{24,28},{26,30},{1,5},{... | collective-permute-start | bytes 786440 | tf_op jit(solution)/shard_map/ppermute | solution.py:261
  29.1 3.5 %collective-permute-done.5.refs_6_ = bf16[256,512]{1,0:T(8,128)(2,1)S(1)} collective-permute-done((bf16[256,512]{1,0:T(8,128)(2,1)S(1)}, bf16[256,512]{1,0:T(8,128)(2,1)S(1)}, u32[]{:S(2)}, u32[]{:S(2)}) %collective-permute-start.5) | collective-permute-done | bytes 262176 | tf_op jit(solution)/shard_map/ppermute | solution.py:249
  32.6 3.1 %collective-permute-start.9 = (bf16[256,512]{1,0:T(8,128)(2,1)S(1)}, bf16[256,512]{1,0:T(8,128)(2,1)}, u32[]{:S(2)}, u32[]{:S(2)}) collective-permute-start(bf16[256,512]{1,0:T(8,128)(2,1)S(1)} %collective-permute-done.5.refs_6_), channel_id=1, source_target_pairs={{24,28},{26,30},{28,24},{30,26},{25,29},{27,31},{29,25},{31,27}} | collective-permute-start | bytes 786440 | tf_op jit(solution)/shard_map/ppermute | solution.py:261
  35.8 8.8 %collective-permute-done.4.refs_5_ = bf16[256,512]{1,0:T(8,128)(2,1)S(1)} collective-permute-done((bf16[256,512]{1,0:T(8,128)(2,1)S(1)}, bf16[256,512]{1,0:T(8,128)(2,1)S(1)}, u32[]{:S(2)}, u32[]{:S(2)}) %collective-permute-start.4) | collective-permute-done | bytes 262176 | tf_op jit(solution)/shard_map/ppermute | solution.py:249
  44.5 3.1 %collective-permute-start.8 = (bf16[256,512]{1,0:T(8,128)(2,1)S(1)}, bf16[256,512]{1,0:T(8,128)(2,1)}, u32[]{:S(2)}, u32[]{:S(2)}) collective-permute-start(bf16[256,512]{1,0:T(8,128)(2,1)S(1)} %collective-permute-done.4.refs_5_), channel_id=1, source_target_pairs={{16,20},{18,22},{20,16},{22,18},{24,28},{26,30},{28,24},{30,26},{1... | collective-permute-start | bytes 786440 | tf_op jit(solution)/shard_map/ppermute | solution.py:261
  47.7 2.1 %collective-permute-start.7 = (bf16[256,512]{1,0:T(8,128)(2,1)S(1)}, bf16[256,512]{1,0:T(8,128)(2,1)}, u32[]{:S(2)}, u32[]{:S(2)}) collective-permute-start(bf16[256,512]{1,0:T(8,128)(2,1)S(1)} %collective-permute-done.3.refs_4_), channel_id=1, source_target_pairs={{8,12},{10,14},{12,8},{14,10},{16,20},{18,22},{20,16},{22,18},{24,... | collective-permute-start | bytes 786440 | tf_op jit(solution)/shard_map/ppermute | solution.py:261
  50.1 5.9 %shard_map.46.refs_0_ = bf16[8,256,128]{2,1,0:T(8,128)(2,1)S(1)} custom-call(s32[1]{0:T(128)} %bitcast.4.which_ref, bf16[64,4096]{1,0:T(8,128)(2,1)S(1)} %copy-done.1, bf16[64,4096]{1,0:T(8,128)(2,1)S(1)} %collective-permute-done.refs_1_, bf16[64,4096]{1,0:T(8,128)(2,1)S(1)} %collective-permute-done.1.refs_2_, ...), custom_call_target="tpu_custom_call" | custom-call | flops 2147483648 | bytes 8388608 | tf_op jit(solution)/shard_map/pallas_call | solution.py:106
  56.0 3.4 %collective-permute-done.7.refs_8_ = bf16[256,512]{1,0:T(8,128)(2,1)} collective-permute-done((bf16[256,512]{1,0:T(8,128)(2,1)S(1)}, bf16[256,512]{1,0:T(8,128)(2,1)}, u32[]{:S(2)}, u32[]{:S(2)}) %collective-permute-start.7) | collective-permute-done | bytes 262176 | tf_op jit(solution)/shard_map/ppermute | solution.py:261
  59.5 9.6 %shard_map.48 = bf16[8,256,128]{2,1,0:T(8,128)(2,1)S(1)} custom-call(s32[7]{0:T(128)S(1)} %stack.29.seen_ref, bf16[8,256,128]{2,1,0:T(8,128)(2,1)S(1)} %shard_map.46.refs_0_, s32[256,1]{1,0:T(8,128)S(1)} %copy.7.refs_1_, s32[1,256]{1,0:T(1,128)S(1)} %bitcast.22, bf16[256,512]{1,0:T(8,128)(2,1)S(1)} %shard_map.47.refs_3_, ...), custom_call_target="tpu_custom_call" | custom-call | flops 2147483648 | bytes 1048576 | tf_op jit(solution)/shard_map/pallas_call | solution.py:186
  69.2 0.2 copy.9
  69.5 1.5 %collective-permute-start.10 = (bf16[128,1024]{1,0:T(8,128)(2,1)S(1)}, bf16[128,1024]{1,0:T(8,128)(2,1)S(1)}, u32[]{:S(2)}, u32[]{:S(2)}) collective-permute-start(bf16[128,1024]{1,0:T(8,128)(2,1)S(1)} %bitcast.25), channel_id=1, source_target_pairs={{0,2},{2,0},{4,6},{6,4},{8,10},{10,8},{12,14},{14,12},{16,18},{18,... | collective-permute-start | bytes 786440 | tf_op jit(solution)/shard_map/ppermute | solution.py:218
  71.1 1.0 %collective-permute-done.10 = bf16[128,1024]{1,0:T(8,128)(2,1)S(1)} collective-permute-done((bf16[128,1024]{1,0:T(8,128)(2,1)S(1)}, bf16[128,1024]{1,0:T(8,128)(2,1)S(1)}, u32[]{:S(2)}, u32[]{:S(2)}) %collective-permute-start.10) | collective-permute-done | bytes 262176 | tf_op jit(solution)/shard_map/ppermute | solution.py:218
  72.2 0.8 %pad_maximum_fusion = bf16[128,2048]{1,0:T(8,128)(2,1)} fusion(bf16[128,1024]{1,0:T(8,128)(2,1)S(1)} %get-tuple-element.8, bf16[128,1024]{1,0:T(8,128)(2,1)S(1)} %get-tuple-element.7), kind=kLoop, calls=%fused_computation.1 | loop fusion | flops 1048576 | bytes 1048576 | tf_op jit(solution)/shard_map/concatenate | solution.py:279
  (22 shorter events, 1.0 us)
Async XLA Ops:
  0.0 13.0 %collective-permute-start.1 = (bf16[64,4096]{1,0:T(8,128)(2,1)}, bf16[64,4096]{1,0:T(8,128)(2,1)S(1)}, u32[]{:S(2)}, u32[]{:S(2)}) collective-permute-start(bf16[64,4096]{1,0:T(8,128)(2,1)} %refs_0_.3), channel_id=1, source_target_pairs={{0,1},{1,0},{2,3},{3,2},{4,5},{5,4},{6,7},{7,6},{8,9},{9,8},{10,11... | collective-permute-start | bytes 1572872 | tf_op jit(solution)/shard_map/ppermute | solution.py:227
  1.2 14.1 %collective-permute-start = (bf16[64,4096]{1,0:T(8,128)(2,1)}, bf16[64,4096]{1,0:T(8,128)(2,1)S(1)}, u32[]{:S(2)}, u32[]{:S(2)}) collective-permute-start(bf16[64,4096]{1,0:T(8,128)(2,1)} %refs_0_.3), channel_id=1, source_target_pairs={{0,2},{2,0},{4,6},{6,4},{8,10},{10,8},{12,14},{14,12},{16,18},{18,... | collective-permute-start | bytes 1572872 | tf_op jit(solution)/shard_map/ppermute | solution.py:218
  13.0 3.1 %collective-permute-start.2 = (bf16[64,4096]{1,0:T(8,128)(2,1)S(1)}, bf16[64,4096]{1,0:T(8,128)(2,1)S(1)}, u32[]{:S(2)}, u32[]{:S(2)}) collective-permute-start(bf16[64,4096]{1,0:T(8,128)(2,1)S(1)} %collective-permute-done.1.refs_2_), channel_id=1, source_target_pairs={{0,2},{2,0},{4,6},{6,4},{8,10},{10,8},{12,14},{14,12},{16,18},{18,... | collective-permute-start | bytes 1572872 | tf_op jit(solution)/shard_map/ppermute | solution.py:218
  16.1 1.0 %copy-start = (bf16[64,4096]{1,0:T(8,128)(2,1)S(1)}, bf16[64,4096]{1,0:T(8,128)(2,1)}, u32[]{:S(2)}) copy-start(bf16[64,4096]{1,0:T(8,128)(2,1)} %refs_0_.3) | copy-start | bytes 1572868
  17.1 33.0 %copy-start.1 = (bf16[64,4096]{1,0:T(8,128)(2,1)S(1)}, bf16[64,4096]{1,0:T(8,128)(2,1)}, u32[]{:S(2)}) copy-start(bf16[64,4096]{1,0:T(8,128)(2,1)} %refs_0_.3) | copy-start | bytes 1572868
  21.3 11.3 %collective-permute-start.5 = (bf16[256,512]{1,0:T(8,128)(2,1)S(1)}, bf16[256,512]{1,0:T(8,128)(2,1)S(1)}, u32[]{:S(2)}, u32[]{:S(2)}) collective-permute-start(bf16[256,512]{1,0:T(8,128)(2,1)S(1)} %shard_map.47.refs_3_), channel_id=1, source_target_pairs={{0,24},{2,26},{4,28},{6,30},{1,25},{3,27},{5,29},{7,31}} | collective-permute-start | bytes 786440 | tf_op jit(solution)/shard_map/ppermute | solution.py:249
  22.6 21.9 %collective-permute-start.4 = (bf16[256,512]{1,0:T(8,128)(2,1)S(1)}, bf16[256,512]{1,0:T(8,128)(2,1)S(1)}, u32[]{:S(2)}, u32[]{:S(2)}) collective-permute-start(bf16[256,512]{1,0:T(8,128)(2,1)S(1)} %shard_map.47.refs_3_), channel_id=1, source_target_pairs={{0,16},{2,18},{4,20},{6,22},{8,24},{10,26},{12,28},{14,30},{1,17},... | collective-permute-start | bytes 786440 | tf_op jit(solution)/shard_map/ppermute | solution.py:249
  23.9 23.8 %collective-permute-start.3 = (bf16[256,512]{1,0:T(8,128)(2,1)S(1)}, bf16[256,512]{1,0:T(8,128)(2,1)S(1)}, u32[]{:S(2)}, u32[]{:S(2)}) collective-permute-start(bf16[256,512]{1,0:T(8,128)(2,1)S(1)} %shard_map.47.refs_3_), channel_id=1, source_target_pairs={{0,8},{2,10},{4,12},{6,14},{8,16},{10,18},{12,20},{14,22},{16,24},... | collective-permute-start | bytes 786440 | tf_op jit(solution)/shard_map/ppermute | solution.py:249
  25.2 30.8 %collective-permute-start.6 = (bf16[256,512]{1,0:T(8,128)(2,1)S(1)}, bf16[256,512]{1,0:T(8,128)(2,1)}, u32[]{:S(2)}, u32[]{:S(2)}) collective-permute-start(bf16[256,512]{1,0:T(8,128)(2,1)S(1)} %shard_map.47.refs_3_), channel_id=1, source_target_pairs={{0,4},{2,6},{8,12},{10,14},{16,20},{18,22},{24,28},{26,30},{1,5},{... | collective-permute-start | bytes 786440 | tf_op jit(solution)/shard_map/ppermute | solution.py:261
  32.6 23.4 %collective-permute-start.9 = (bf16[256,512]{1,0:T(8,128)(2,1)S(1)}, bf16[256,512]{1,0:T(8,128)(2,1)}, u32[]{:S(2)}, u32[]{:S(2)}) collective-permute-start(bf16[256,512]{1,0:T(8,128)(2,1)S(1)} %collective-permute-done.5.refs_6_), channel_id=1, source_target_pairs={{24,28},{26,30},{28,24},{30,26},{25,29},{27,31},{29,25},{31,27}} | collective-permute-start | bytes 786440 | tf_op jit(solution)/shard_map/ppermute | solution.py:261
  44.5 11.5 %collective-permute-start.8 = (bf16[256,512]{1,0:T(8,128)(2,1)S(1)}, bf16[256,512]{1,0:T(8,128)(2,1)}, u32[]{:S(2)}, u32[]{:S(2)}) collective-permute-start(bf16[256,512]{1,0:T(8,128)(2,1)S(1)} %collective-permute-done.4.refs_5_), channel_id=1, source_target_pairs={{16,20},{18,22},{20,16},{22,18},{24,28},{26,30},{28,24},{30,26},{1... | collective-permute-start | bytes 786440 | tf_op jit(solution)/shard_map/ppermute | solution.py:261
  47.7 11.8 %collective-permute-start.7 = (bf16[256,512]{1,0:T(8,128)(2,1)S(1)}, bf16[256,512]{1,0:T(8,128)(2,1)}, u32[]{:S(2)}, u32[]{:S(2)}) collective-permute-start(bf16[256,512]{1,0:T(8,128)(2,1)S(1)} %collective-permute-done.3.refs_4_), channel_id=1, source_target_pairs={{8,12},{10,14},{12,8},{14,10},{16,20},{18,22},{20,16},{22,18},{24,... | collective-permute-start | bytes 786440 | tf_op jit(solution)/shard_map/ppermute | solution.py:261
  69.5 2.6 %collective-permute-start.10 = (bf16[128,1024]{1,0:T(8,128)(2,1)S(1)}, bf16[128,1024]{1,0:T(8,128)(2,1)S(1)}, u32[]{:S(2)}, u32[]{:S(2)}) collective-permute-start(bf16[128,1024]{1,0:T(8,128)(2,1)S(1)} %bitcast.25), channel_id=1, source_target_pairs={{0,2},{2,0},{4,6},{6,4},{8,10},{10,8},{12,14},{14,12},{16,18},{18,... | collective-permute-start | bytes 786440 | tf_op jit(solution)/shard_map/ppermute | solution.py:218

commit v2 on v1

v2 whole, which is shorter than its diff:
```python
import functools
import math

import jax
import jax.numpy as jnp
from jax import lax
from jax.experimental import pallas as pl
from jax.experimental.pallas import tpu as pltpu
from jax.sharding import PartitionSpec as P

HD = 128
THETA = 500000.0
NEGATIVE = -1e30
HALF, OUTER, INNER, FACTS = 0, 1, 2, 3
VMEM = pl.BlockSpec(memory_space=pltpu.VMEM)


def tables(positions):
    frequency = THETA ** (-(jnp.arange(HD // 2).astype(jnp.float32) * 2.0 / HD))
    angles = positions.astype(jnp.float32)[:, None] * frequency[None, :]
    cosine, sine = jnp.cos(angles), jnp.sin(angles)
    return jnp.concatenate([cosine, cosine], axis=1), jnp.concatenate([-sine, sine], axis=1)


def turn(head, cosine, sine):
    return head * cosine + pltpu.roll(head, HD // 2, 1) * sine


def write_kv(product, cosine, sine, out_ref):
    width = product.shape[1] // 2
    for at in range(0, width, HD):
        cut = slice(at, at + HD)
        out_ref[:, cut] = turn(product[:, cut], cosine[...], sine[...]).astype(jnp.bfloat16)
    out_ref[:, width:] = product[:, width:].astype(jnp.bfloat16)


def first_kernel(parts, chunks, facts_ref, *refs):
    rows_in = refs[:parts]
    key_w, value_w, query_w, cosine, sine = refs[parts : parts + 5]
    out_ref, rows_ref, kv_ref, q_ref, kv_sem, q_sem, row_sem = refs[parts + 5 :]
    model = key_w.shape[0]
    depth = model // chunks
    width = kv_ref.shape[1] // 2
    wide = q_ref.shape[1]
    half = facts_ref[HALF]
    narrow_at = pl.multiple_of(half * width, width)
    wide_at = pl.multiple_of(half * wide, wide)
    count = rows_in[0].shape[0]
    own = pltpu.make_async_copy(rows_in[0], rows_ref.at[pl.ds(0, count)], row_sem)
    small, large = [], []
    for i in range(chunks):
        cut = pl.ds(i * depth, depth)
        for j, source in enumerate((key_w, value_w)):
            small.append(
                pltpu.make_async_copy(
                    source.at[cut, pl.ds(narrow_at, width)],
                    kv_ref.at[cut, pl.ds(j * width, width)],
                    kv_sem.at[i, j],
                )
            )
        large.append(
            pltpu.make_async_copy(
                query_w.at[cut, pl.ds(wide_at, wide)], q_ref.at[cut, :], q_sem.at[i]
            )
        )
    for copy in [own] + small + large:
        copy.start()
    for i in range(1, parts):
        rows_ref[i * count : (i + 1) * count, :] = rows_in[i][...]
    own.wait()
    product = None
    for i in range(chunks):
        small[2 * i].wait()
        small[2 * i + 1].wait()
        cut = slice(i * depth, (i + 1) * depth)
        term = jnp.dot(rows_ref[:, cut], kv_ref[cut, :], preferred_element_type=jnp.float32)
        product = term if product is None else product + term
    write_kv(product, cosine, sine, out_ref)
    for copy in large:
        copy.wait()


def later_kernel(parts, *refs):
    rows_in = refs[:parts]
    weight, cosine, sine, out_ref, rows_ref = refs[parts:]
    at = 0
    for r in rows_in:
        rows_ref[at : at + r.shape[0], :] = r[...]
        at += r.shape[0]
    product = jnp.dot(rows_ref[...], weight[...], preferred_element_type=jnp.float32)
    write_kv(product, cosine, sine, out_ref)


def query_kernel(parts, *refs):
    rows_in = refs[:parts]
    weight, cosine, sine, out_ref = refs[parts:]
    rows = jnp.concatenate([r[...] for r in rows_in], axis=0)
    heads = out_ref.shape[0]
    step = math.gcd(heads, 2)
    for at in range(0, heads, step):
        product = jnp.dot(
            rows, weight[:, at * HD : (at + step) * HD], preferred_element_type=jnp.float32
        )
        for h in range(step):
            head = product[:, h * HD : (h + 1) * HD]
            out_ref[at + h] = turn(head, cosine[...], sine[...]).astype(jnp.bfloat16)


SMEM = pl.BlockSpec(memory_space=pltpu.SMEM)
FAR = pl.BlockSpec(memory_space=pltpu.HBM)


def close(array):
    return pltpu.with_memory_space_constraint(array, pltpu.VMEM)


def params(megabytes):
    return pltpu.CompilerParams(vmem_limit_bytes=megabytes * 1024 * 1024)


def project_first(facts, blocks, key_weight, value_weight, query_weight, cosine, sine, kv_heads, heads):
    rows = sum(b.shape[0] for b in blocks)
    model = key_weight.shape[0]
    width = kv_heads * HD
    chunks = 4
    far = lambda a: pltpu.with_memory_space_constraint(a, pltpu.HBM)
    return pl.pallas_call(
        functools.partial(first_kernel, len(blocks), chunks),
        out_shape=[
            jax.ShapeDtypeStruct((rows, 2 * width), jnp.bfloat16),
            pltpu.VMEM((rows, model), jnp.bfloat16),
            pltpu.VMEM((model, 2 * width), jnp.bfloat16),
            pltpu.VMEM((model, heads * HD), jnp.bfloat16),
        ],
        in_specs=[SMEM, FAR] + [VMEM] * (len(blocks) - 1) + [FAR] * 3 + [VMEM] * 2,
        out_specs=[VMEM] * 4,
        scratch_shapes=[
            pltpu.SemaphoreType.DMA((chunks, 2)),
            pltpu.SemaphoreType.DMA((chunks,)),
            pltpu.SemaphoreType.DMA(()),
        ],
        compiler_params=params(24),
        cost_estimate=pl.CostEstimate(
            flops=4 * rows * model * width,
            bytes_accessed=2 * model * (heads * HD + 2 * width),
            transcendentals=0,
        ),
    )(facts, far(blocks[0]), *blocks[1:], far(key_weight), far(value_weight), far(query_weight), cosine, sine)


def project_later(blocks, weight, cosine, sine):
    rows = sum(b.shape[0] for b in blocks)
    return pl.pallas_call(
        functools.partial(later_kernel, len(blocks)),
        out_shape=[
            jax.ShapeDtypeStruct((rows, weight.shape[1]), jnp.bfloat16),
            pltpu.VMEM((rows, weight.shape[0]), jnp.bfloat16),
        ],
        in_specs=[VMEM] * (len(blocks) + 3),
        out_specs=[VMEM] * 2,
        compiler_params=params(24),
        cost_estimate=pl.CostEstimate(
            flops=2 * rows * weight.size, bytes_accessed=2 * weight.size, transcendentals=0
        ),
    )(*blocks, close(weight), cosine, sine)


def project_q(blocks, weight, cosine, sine, heads):
    rows = sum(b.shape[0] for b in blocks)
    return pl.pallas_call(
        functools.partial(query_kernel, len(blocks)),
        out_shape=jax.ShapeDtypeStruct((heads, rows, HD), jnp.bfloat16),
        in_specs=[VMEM] * (len(blocks) + 3),
        out_specs=VMEM,
        compiler_params=params(24),
        cost_estimate=pl.CostEstimate(
            flops=2 * rows * weight.size, bytes_accessed=2 * weight.size, transcendentals=0
        ),
    )(*[close(b) for b in blocks], close(weight), cosine, sine)


def attend_kernel(first, last, own_count, origins, kv_heads, pair, block_rows, facts_ref, *refs):
    refs = list(refs)
    query_ref = refs.pop(0)
    far_count = len(origins)
    own, far = refs[:own_count], refs[own_count : own_count + far_count]
    refs = refs[own_count + far_count :]
    if not first:
        top_in, total_in, sum_in = refs[:3]
        refs = refs[3:]
    heads, rows, _ = query_ref.shape
    group = heads // kv_heads
    factor = math.log2(math.e) / math.sqrt(HD)
    hidden = [
        jnp.where(facts_ref[OUTER if hop else INNER] >= (hop or turn_by), 0.0, -NEGATIVE)
        for hop, turn_by in origins
    ]
    blocks = rows // block_rows

    def position(index):
        result = facts_ref[FACTS + blocks] + index
        for i in range(1, blocks):
            start = facts_ref[FACTS + blocks + i] - i * block_rows
            result = jnp.where(index >= i * block_rows, start + index, result)
        return result

    if own_count:
        query_pos = position(lax.broadcasted_iota(jnp.int32, (rows, 1), 0))
        key_pos = position(lax.broadcasted_iota(jnp.int32, (1, rows), 1))

    def lane_max(block):
        if block.shape[1] % HD:
            return jnp.broadcast_to(jnp.max(block, axis=1, keepdims=True), (rows, HD))
        return functools.reduce(jnp.maximum, [block[:, i : i + HD] for i in range(0, block.shape[1], HD)])

    def lane_sum(block):
        if block.shape[1] % HD:
            whole = jnp.sum(block, axis=1, keepdims=True)
            return jnp.where(lax.broadcasted_iota(jnp.int32, (rows, HD), 1) == 0, whole, 0.0)
        return functools.reduce(jnp.add, [block[:, i : i + HD] for i in range(0, block.shape[1], HD)])

    for kv_head in range(kv_heads):
        key_cut = slice(kv_head * HD, (kv_head + 1) * HD)
        value_cut = slice((kv_heads + kv_head) * HD, (kv_heads + kv_head + 1) * HD)
        for member in range(group):
            head = kv_head * group + member
            query = query_ref[head]
            scores = []
            for r in own + far:
                scores.append(
                    lax.dot_general(
                        query, r[:, key_cut], (((1,), (1,)), ((), ())), preferred_element_type=jnp.float32
                    )
                )
            at = 0
            for i, r in enumerate(own):
                allowed = key_pos[:, at : at + r.shape[0]] <= query_pos
                scores[i] = jnp.where(allowed, scores[i], NEGATIVE)
                at += r.shape[0]
            bias = [0.0] * own_count + hidden
            top = None if first else top_in[head]
            for block, shift in zip(scores, bias):
                best = lane_max(block) - shift
                top = best if top is None else jnp.maximum(top, best)
            top = jnp.max(top, axis=1, keepdims=True)
            limit = top * factor
            if first:
                total = result = None
            else:
                before = jnp.exp2(top_in[head] * factor - limit)
                total = total_in[head] * before
                result = sum_in[head] * before
            for block, shift, r in zip(scores, bias, own + far):
                weights = jnp.exp2(block * factor - (limit + shift))
                part = lane_sum(weights)
                term = jnp.dot(
                    weights.astype(jnp.bfloat16), r[:, value_cut], preferred_element_type=jnp.float32
                )
                total = part if total is None else total + part
                result = term if result is None else result + term
            if not last:
                refs[0][head] = jnp.broadcast_to(top, (rows, HD))
                refs[1][head] = total
                refs[2][head] = result
            else:
                result = (result / jnp.sum(total, axis=1, keepdims=True)).astype(jnp.bfloat16)
                column = slice(head * HD, (head + 1) * HD)
                for i in range(blocks):
                    to = pl.multiple_of(facts_ref[FACTS + i] * block_rows, block_rows)
                    refs[i % pair][pl.ds(to, block_rows), column] = result[
                        i * block_rows : (i + 1) * block_rows
                    ]


def attend(facts, queries, own, far, origins, state, last, kv_heads, pair, block_rows):
    heads, rows, _ = queries.shape
    first = state is None
    keys = sum(r.shape[0] for r in own) + sum(r.shape[0] for r in far)
    held = jax.ShapeDtypeStruct((heads, rows, HD), jnp.float32)
    done = jax.ShapeDtypeStruct((rows // pair, heads * HD), jnp.bfloat16)
    operands = [queries] + list(own) + list(far) + ([] if first else list(state))
    return pl.pallas_call(
        functools.partial(attend_kernel, first, last, len(own), origins, kv_heads, pair, block_rows),
        out_shape=[done] * pair if last else [held] * 3,
        in_specs=[SMEM] + [VMEM] * len(operands),
        out_specs=[VMEM] * (pair if last else 3),
        compiler_params=params(24),
        cost_estimate=pl.CostEstimate(
            flops=4 * heads * rows * keys * HD,
            bytes_accessed=heads * rows * HD * 4,
            transcendentals=heads * rows * keys,
        ),
    )(facts, *operands)


def join_kernel(facts_ref, mine, theirs, out_ref):
    width = mine.shape[1]
    to = facts_ref[HALF] * width
    out_ref[:, pl.ds(pl.multiple_of(to, width), width)] = mine[...]
    out_ref[:, pl.ds(pl.multiple_of(width - to, width), width)] = theirs[...]


def local(activations, query_weight, key_weight, value_weight):
    tensor_count, context_count = lax.axis_size("tp"), lax.axis_size("ctx")
    tensor_index, context_index = lax.axis_index("tp"), lax.axis_index("ctx")
    rows_here = activations.shape[0]
    local_rows = rows_here * tensor_count
    heads_here = query_weight.shape[1] // HD
    kv_here = key_weight.shape[1] // HD
    pair = 2 if context_count % 2 == 0 and kv_here % 2 == 0 else 1
    kv_heads, heads = kv_here // pair, heads_here // pair
    places = context_count // pair
    inner = 2 ** (int(math.log2(places)) // 2) if places & (places - 1) == 0 else 1
    outer = places // inner
    half = context_index % pair
    place = context_index // pair
    far_out, far_in = place // inner, place % inner

    def swap(block):
        return lax.ppermute(block, "ctx", [(i, i ^ 1) for i in range(context_count)])

    def device(o, i, c):
        return (o * inner + i) * pair + c

    blocks, owners = [activations], [tensor_index]
    for shift in range(1, tensor_count):
        links = [(i, (i + shift) % tensor_count) for i in range(tensor_count)]
        blocks.append(lax.ppermute(activations, "tp", links))
        owners.append((tensor_index - shift) % tensor_count)
    owners = [owner for owner in owners for c in range(pair)]
    starts = [
        (place * pair + (half + i % pair) % pair) * local_rows + owner * rows_here
        for i, owner in enumerate(owners)
    ]
    facts = jnp.stack([half, far_out, far_in] + owners + starts).astype(jnp.int32)
    positions = jnp.concatenate([s + jnp.arange(rows_here, dtype=jnp.int32) for s in starts])
    cosine, sine = tables(positions)

    def after(value, others):
        return lax.optimization_barrier((value, list(others)))[0] if others else value

    def after(value, others):
        return lax.optimization_barrier((value, list(others)))[0] if others else value

    def both(wave):
        return [b if c == 0 else swap(b) for b in wave for c in range(pair)]

    hops = range(1, outer)

    def upward(piece):
        columns = {}
        for hop in hops:
            links = [
                (device(o, i, c), device(o + hop, i, c))
                for o in range(outer - hop)
                for i in range(inner)
                for c in range(pair)
            ]
            columns[hop] = lax.ppermute(piece, "ctx", links)
        return columns

    def aside(block, first, parts=(0,)):
        moved = []
        for turn_by in range(1, inner):
            links = [
                (device(o, i, c), device(o, (i + turn_by) % inner, c))
                for o in range(first, outer)
                for i in range(inner)
                for c in range(pair)
                if first > 0 or i + turn_by < inner
            ]
            block_in = lax.ppermute(block, "ctx", links)
            for part, hop in zip(jnp.split(block_in, len(parts)), parts):
                moved.append((part, (hop, turn_by)))
        return moved

    state = None

    def fold(own, pieces, last):
        nonlocal state
        limit = max(1, (1024 - local_rows) // max([block.shape[0] for block, _ in pieces] + [1]))
        for i in range(0, max(1, len(pieces)), limit):
            some = pieces[i : i + limit]
            state = attend(
                facts, queries, own if i == 0 else [], [block for block, _ in some], [o for _, o in some],
                state, last and i + limit >= len(pieces), kv_heads, pair, rows_here,
            )

    held = both(blocks[:1])
    count = len(held) * rows_here
    first, first_rows, kv_weight, q_weight = project_first(
        facts, held, key_weight, value_weight, query_weight, cosine[:count], sine[:count], kv_heads, heads
    )
    columns = upward(first)
    beside = aside(first, 0)
    early = [hop for hop in hops if hop != 2]
    gate = [columns[hop] for hop in early] + [b for b, _ in beside]
    late = both([after(b, gate) for b in blocks[1:]])
    second, second_rows = project_later(late, kv_weight, cosine[count:], sine[count:])
    pieces = [(columns[hop], (hop, 0)) for hop in hops] + beside
    if early:
        pieces += aside(jnp.concatenate([columns[hop] for hop in early], axis=0), 1, early)
    later = upward(second)
    more = [(later[hop], (hop, 0)) for hop in hops] + aside(second, 0)
    queries = project_q([first_rows, second_rows], q_weight, cosine, sine, heads)
    if early:
        block, parts = later[1], [1]
        if outer > 2:
            block, parts = jnp.concatenate([later[1], columns[2]], axis=0), [1, 2]
        more += aside(after(block, [queries]), 1, parts)
    fold([first, second], pieces, False)
    last = [m for hop in hops if hop > 1 for m in aside(after(later[hop], state[:1]), hop, [hop])]
    fold([], more, not last)
    if last:
        fold([], last, True)
    if pair == 1:
        return state[0]
    return pl.pallas_call(
        join_kernel,
        out_shape=jax.ShapeDtypeStruct((local_rows, pair * heads * HD), jnp.bfloat16),
        in_specs=[pl.BlockSpec(memory_space=pltpu.SMEM), VMEM, VMEM],
        out_specs=VMEM,
        compiler_params=params(4),
    )(facts, state[0], swap(state[1]))


def solution(mesh):
    in_specs = (P(("ctx", "tp"), None), P(None, "tp"), P(None, "tp"), P(None, "tp"))
    return jax.shard_map(local, mesh=mesh, in_specs=in_specs, out_specs=P("ctx", "tp"), check_vma=False)
```

time: 73.5 us -> 58.8 us (0.80)
  waiting for transfers between devices: 28.2 us -> 7.25 us
  starting transfers between devices: 21.3 us -> 29.5 us
  local copies, waits for them, and re-layouts: 1.72 us -> 0.13 us
  other arithmetic: 1.85 us -> 1.07 us
    ppermute x8 -> x13, waiting for transfers between devices: 26.5 us -> 6.08 us  [the longest x6 5.69 us: upward(): columns[hop] = lax.ppermute(piece, 'ctx', links)]
    ppermute x8 -> x13, starting transfers between devices: 17.4 us -> 26 us  [the longest x6 17 us: aside(): block_in = lax.ppermute(block, 'ctx', links)]
    pallas_call x2 -> x6, Pallas kernels: 13.8 us -> 17.7 us  [the longest x3 10 us: attend(): pl.pallas_call(functools.partial(attend_kernel, first, last, len(own), or...]
    pallas_call x1, Pallas kernels: 5.87 us -> 2.48 us  [project_q(): pl.pallas_call(functools.partial(query_kernel, len(blocks)), out_shape=ja...]
    unnamed x5 -> x0, local copies, waits for them, and re-layouts: 1.09 us -> none
    concatenate x1 -> x2, other arithmetic: 0.83 us -> 0.04 us  [the longest x1 0.02 us: local(): jnp.concatenate([columns[hop] for hop in early], axis=0)]
  transfers between devices with their start and end apart: 11 -> 16, of which waited for: 6 -> 6; matrix products, arithmetic and copies ran while one was open for 2% -> 2% of each run, Pallas kernels for 8% -> 29%
where the time goes in v2:
time: 58.8 us; the launch traced here: 58.5 us
  starting transfers between devices  29.5 us (50%)
  Pallas kernels  20.2 us (34%)
  waiting for transfers between devices  7.25 us (12%)
  other arithmetic  1.07 us (2%)
    ppermute x6, starting transfers between devices, aside(): block_in = lax.ppermute(block, 'ctx', links)  17 us
    pallas_call x3, Pallas kernels, attend(): pl.pallas_call(functools.partial(attend_kernel, first, last, len(own), or...  10 us
    ppermute x6, starting transfers between devices, upward(): columns[hop] = lax.ppermute(piece, 'ctx', links)  7.75 us
    ppermute x6, waiting for transfers between devices, upward(): columns[hop] = lax.ppermute(piece, 'ctx', links)  5.69 us
    pallas_call x1, Pallas kernels, project_first(): pl.pallas_call(functools.partial(first_kernel, len(blocks), chunks), out_...  5.51 us
    ppermute x3, starting transfers between devices, swap(): lax.ppermute(block, 'ctx', [(i, i ^ 1) for i in range(context_count)])  3.51 us
    pallas_call x1, Pallas kernels, project_q(): pl.pallas_call(functools.partial(query_kernel, len(blocks)), out_shape=ja...  2.48 us
    pallas_call x1, Pallas kernels, local(): pl.pallas_call(join_kernel, out_shape=jax.ShapeDtypeStruct((local_rows, p...  1.37 us
  transfers between devices with their start and end apart: 16, of which 6 were waited for; matrix products, arithmetic and copies ran while one was open for 2% of the time, Pallas kernels for 29%

profile of v2, /device:TPU:25, one launch (start us, length us, event | category | flops | bytes accessed | tf_op | source)
XLA Modules:
  0.0 58.5 jit_solution(8048401303249534050)
XLA Ops:
  0.7 1.2 %collective-permute-start.1 = (bf16[64,4096]{1,0:T(8,128)(2,1)}, bf16[64,4096]{1,0:T(8,128)(2,1)S(1)}, u32[]{:S(2)}, u32[]{:S(2)}) collective-permute-start(bf16[64,4096]{1,0:T(8,128)(2,1)} %refs_0_.1), channel_id=1, source_target_pairs={{0,1},{1,0},{2,3},{3,2},{4,5},{5,4},{6,7},{7,6},{8,9},{9,8},{10,11... | collective-permute-start | bytes 1572872 | tf_op jit(solution)/shard_map/ppermute | solution.py:328
  2.9 5.5 %shard_map.46 = (bf16[128,512]{1,0:T(8,128)(2,1)S(1)}, bf16[128,4096]{1,0:T(8,128)(2,1)S(1)}, bf16[4096,512]{1,0:T(8,128)(2,1)S(1)}, bf16[4096,1024]{1,0:T(8,128)(2,1)S(1)}) custom-call(s32[11]{0:T(128)S(1)} %stack.41.facts_ref, bf16[64,4096]{1,0:T(8,128)(2,1)} %refs_0_.1, bf16[64,4096]{1,0:T(8,128)(2,1)S(1)} %collective-permute-done.refs_1_, ...), custom_call_target="tpu_custom_call" | custom-call | flops 536870912 | bytes 12582912 | tf_op jit(solution)/shard_map/pallas_call | solution.py:127
  8.4 1.3 %collective-permute-start.2 = (bf16[128,512]{1,0:T(8,128)(2,1)S(1)}, bf16[128,512]{1,0:T(8,128)(2,1)S(1)}, u32[]{:S(2)}, u32[]{:S(2)}) collective-permute-start(bf16[128,512]{1,0:T(8,128)(2,1)S(1)} %get-tuple-element.24.refs_1_), channel_id=1, source_target_pairs={{0,8},{2,10},{4,12},{6,14},{8,16},{10,18},{12,20},{14,22},{16,24},... | collective-permute-start | bytes 393224 | tf_op jit(solution)/shard_map/ppermute | solution.py:359
  9.7 1.3 %collective-permute-start.3 = (bf16[128,512]{1,0:T(8,128)(2,1)S(1)}, bf16[128,512]{1,0:T(8,128)(2,1)S(1)}, u32[]{:S(2)}, u32[]{:S(2)}) collective-permute-start(bf16[128,512]{1,0:T(8,128)(2,1)S(1)} %get-tuple-element.24.refs_1_), channel_id=1, source_target_pairs={{0,24},{2,26},{4,28},{6,30},{1,25},{3,27},{5,29},{7,31}} | collective-permute-start | bytes 393224 | tf_op jit(solution)/shard_map/ppermute | solution.py:359
  11.0 3.2 %collective-permute-start.4 = (bf16[128,512]{1,0:T(8,128)(2,1)S(1)}, bf16[128,512]{1,0:T(8,128)(2,1)S(1)}, u32[]{:S(2)}, u32[]{:S(2)}) collective-permute-start(bf16[128,512]{1,0:T(8,128)(2,1)S(1)} %get-tuple-element.24.refs_1_), channel_id=1, source_target_pairs={{0,4},{2,6},{8,12},{10,14},{16,20},{18,22},{24,28},{26,30},{1,5},{... | collective-permute-start | bytes 393224 | tf_op jit(solution)/shard_map/ppermute | solution.py:372
  15.1 3.1 %collective-permute-done.3.refs_5_ = bf16[128,512]{1,0:T(8,128)(2,1)S(1)} collective-permute-done((bf16[128,512]{1,0:T(8,128)(2,1)S(1)}, bf16[128,512]{1,0:T(8,128)(2,1)S(1)}, u32[]{:S(2)}, u32[]{:S(2)}) %collective-permute-start.3) | collective-permute-done | bytes 131104 | tf_op jit(solution)/shard_map/ppermute | solution.py:359
  18.2 1.1 %collective-permute-start.5 = (bf16[64,4096]{1,0:T(8,128)(2,1)S(1)}, bf16[64,4096]{1,0:T(8,128)(2,1)S(1)}, u32[]{:S(2)}, u32[]{:S(2)}) collective-permute-start(bf16[64,4096]{1,0:T(8,128)(2,1)S(1)} %collective-permute-done.1.refs_0_), channel_id=1, source_target_pairs={{0,2},{2,0},{4,6},{6,4},{8,10},{10,8},{12,14},{14,12},{16,18},{18,... | collective-permute-start | bytes 1572872 | tf_op jit(solution)/shard_map/ppermute | solution.py:320
  19.5 1.3 %collective-permute-start.7 = (bf16[128,512]{1,0:T(8,128)(2,1)S(1)}, bf16[128,512]{1,0:T(8,128)(2,1)S(1)}, u32[]{:S(2)}, u32[]{:S(2)}) collective-permute-start(bf16[128,512]{1,0:T(8,128)(2,1)S(1)} %get-tuple-element.24.refs_1_), channel_id=1, source_target_pairs={{0,16},{2,18},{4,20},{6,22},{8,24},{10,26},{12,28},{14,30},{1,17},... | collective-permute-start | bytes 393224 | tf_op jit(solution)/shard_map/ppermute | solution.py:359
  20.8 3.1 %collective-permute-start.8 = (bf16[256,512]{1,0:T(8,128)(2,1)S(1)}, bf16[256,512]{1,0:T(8,128)(2,1)S(1)}, u32[]{:S(2)}, u32[]{:S(2)}) collective-permute-start(bf16[256,512]{1,0:T(8,128)(2,1)S(1)} %pad_maximum_fusion), channel_id=1, source_target_pairs={{8,12},{10,14},{12,8},{14,10},{16,20},{18,22},{20,16},{22,18},{24,... | collective-permute-start | bytes 786440 | tf_op jit(solution)/shard_map/ppermute | solution.py:372
  24.8 1.3 %collective-permute-start.12 = (bf16[128,512]{1,0:T(8,128)(2,1)S(1)}, bf16[128,512]{1,0:T(8,128)(2,1)S(1)}, u32[]{:S(2)}, u32[]{:S(2)}) collective-permute-start(bf16[128,512]{1,0:T(8,128)(2,1)S(1)} %get-tuple-element.29.refs_2_), channel_id=1, source_target_pairs={{0,8},{2,10},{4,12},{6,14},{8,16},{10,18},{12,20},{14,22},{16,24},... | collective-permute-start | bytes 393224 | tf_op jit(solution)/shard_map/ppermute | solution.py:359
  26.1 1.3 %collective-permute-start.10 = (bf16[128,512]{1,0:T(8,128)(2,1)S(1)}, bf16[128,512]{1,0:T(8,128)(2,1)S(1)}, u32[]{:S(2)}, u32[]{:S(2)}) collective-permute-start(bf16[128,512]{1,0:T(8,128)(2,1)S(1)} %get-tuple-element.29.refs_2_), channel_id=1, source_target_pairs={{0,24},{2,26},{4,28},{6,30},{1,25},{3,27},{5,29},{7,31}} | collective-permute-start | bytes 393224 | tf_op jit(solution)/shard_map/ppermute | solution.py:359
  27.4 1.3 %collective-permute-start.6 = (bf16[128,512]{1,0:T(8,128)(2,1)S(1)}, bf16[128,512]{1,0:T(8,128)(2,1)S(1)}, u32[]{:S(2)}, u32[]{:S(2)}) collective-permute-start(bf16[128,512]{1,0:T(8,128)(2,1)S(1)} %get-tuple-element.29.refs_2_), channel_id=1, source_target_pairs={{0,16},{2,18},{4,20},{6,22},{8,24},{10,26},{12,28},{14,30},{1,17},... | collective-permute-start | bytes 393224 | tf_op jit(solution)/shard_map/ppermute | solution.py:359
  28.7 2.5 %shard_map.48.refs_0_ = bf16[8,256,128]{2,1,0:T(8,128)(2,1)S(1)} custom-call(bf16[128,4096]{1,0:T(8,128)(2,1)S(1)} %get-tuple-element.23.refs_0_, bf16[128,4096]{1,0:T(8,128)(2,1)S(1)} %get-tuple-element.27.refs_1_, bf16[4096,1024]{1,0:T(8,128)(2,1)S(1)} %get-tuple-element.28.refs_2_, f32[256,128]{1,0:T(8,128)S(1)} %pad_maximum_fusion.2.refs_3_, ...), custom_call_target="tpu_custom_call" | custom-call | flops 2147483648 | bytes 8388608 | tf_op jit(solution)/shard_map/pallas_call | solution.py:170
  31.2 1.9 %collective-permute-done.12.refs_1_ = bf16[128,512]{1,0:T(8,128)(2,1)S(1)} collective-permute-done((bf16[128,512]{1,0:T(8,128)(2,1)S(1)}, bf16[128,512]{1,0:T(8,128)(2,1)S(1)}, u32[]{:S(2)}, u32[]{:S(2)}) %collective-permute-start.12) | collective-permute-done | bytes 131104 | tf_op jit(solution)/shard_map/ppermute | solution.py:359
  33.1 3.0 %collective-permute-start.14 = (bf16[256,512]{1,0:T(8,128)(2,1)S(1)}, bf16[256,512]{1,0:T(8,128)(2,1)S(1)}, u32[]{:S(2)}, u32[]{:S(2)}) collective-permute-start(bf16[256,512]{1,0:T(8,128)(2,1)S(1)} %pad_maximum_fusion.1), channel_id=1, source_target_pairs={{8,12},{10,14},{12,8},{14,10},{16,20},{18,22},{20,16},{22,18},{24,... | collective-permute-start | bytes 786440 | tf_op jit(solution)/shard_map/ppermute | solution.py:372
  36.2 2.3 %collective-permute-start.13 = (bf16[128,512]{1,0:T(8,128)(2,1)S(1)}, bf16[128,512]{1,0:T(8,128)(2,1)S(1)}, u32[]{:S(2)}, u32[]{:S(2)}) collective-permute-start(bf16[128,512]{1,0:T(8,128)(2,1)S(1)} %get-tuple-element.29.refs_2_), channel_id=1, source_target_pairs={{0,4},{2,6},{8,12},{10,14},{16,20},{18,22},{24,28},{26,30},{1,5},{... | collective-permute-start | bytes 393224 | tf_op jit(solution)/shard_map/ppermute | solution.py:372
  38.5 4.3 %shard_map.49 = (f32[8,256,128]{2,1,0:T(8,128)S(1)}, f32[8,256,128]{2,1,0:T(8,128)S(1)}, f32[8,256,128]{2,1,0:T(8,128)S(1)}) custom-call(s32[11]{0:T(128)S(1)} %stack.41.facts_ref, bf16[8,256,128]{2,1,0:T(8,128)(2,1)S(1)} %shard_map.48.refs_0_, bf16[128,512]{1,0:T(8,128)(2,1)S(1)} %get-tuple-element.24.refs_1_, ...), custom_call_target="tpu_custom_call" | custom-call | flops 1073741824 | bytes 1048576 | tf_op jit(solution)/shard_map/pallas_call | solution.py:282
  42.8 1.9 %collective-permute-start.11 = (bf16[128,512]{1,0:T(8,128)(2,1)S(1)}, bf16[128,512]{1,0:T(8,128)(2,1)S(1)}, u32[]{:S(2)}, u32[]{:S(2)}) collective-permute-start(bf16[128,512]{1,0:T(8,128)(2,1)S(1)} %collective-permute-done.10.refs_3_), channel_id=1, source_target_pairs={{24,28},{26,30},{28,24},{30,26},{25,29},{27,31},{29,25},{31,27}} | collective-permute-start | bytes 393224 | tf_op jit(solution)/shard_map/ppermute | solution.py:372
  44.8 3.5 %collective-permute-start.9 = (bf16[128,512]{1,0:T(8,128)(2,1)S(1)}, bf16[128,512]{1,0:T(8,128)(2,1)S(1)}, u32[]{:S(2)}, u32[]{:S(2)}) collective-permute-start(bf16[128,512]{1,0:T(8,128)(2,1)S(1)} %collective-permute-done.6.refs_2_), channel_id=1, source_target_pairs={{16,20},{18,22},{20,16},{22,18},{24,28},{26,30},{28,24},{30,26},{1... | collective-permute-start | bytes 393224 | tf_op jit(solution)/shard_map/ppermute | solution.py:372
  48.4 3.7 %shard_map.50 = (f32[8,256,128]{2,1,0:T(8,128)S(1)}, f32[8,256,128]{2,1,0:T(8,128)S(1)}, f32[8,256,128]{2,1,0:T(8,128)S(1)}) custom-call(s32[11]{0:T(128)S(1)} %stack.41.facts_ref, bf16[8,256,128]{2,1,0:T(8,128)(2,1)S(1)} %shard_map.48.refs_0_, bf16[128,512]{1,0:T(8,128)(2,1)S(1)} %collective-permute-done.12.refs_1_, ...), custom_call_target="tpu_custom_call" | custom-call | flops 805306368 | bytes 1048576 | tf_op jit(solution)/shard_map/pallas_call | solution.py:282
  52.2 2.0 %shard_map.51 = (bf16[128,1024]{1,0:T(8,128)(2,1)S(1)}, bf16[128,1024]{1,0:T(8,128)(2,1)S(1)}) custom-call(s32[11]{0:T(128)S(1)} %stack.41.facts_ref, bf16[8,256,128]{2,1,0:T(8,128)(2,1)S(1)} %shard_map.48.refs_0_, bf16[128,512]{1,0:T(8,128)(2,1)S(1)} %collective-permute-done.9.refs_1_, bf16[128,512]{1,0:T(8,128)(2,1)S(1)} %collective-permute-done.11.refs_2_, ...), custom_call_target="tpu_custom_call" | custom-call | flops 268435456 | bytes 1048576 | tf_op jit(solution)/shard_map/pallas_call | solution.py:282
  54.2 1.7 %collective-permute-start.15 = (bf16[128,1024]{1,0:T(8,128)(2,1)S(1)}, bf16[128,1024]{1,0:T(8,128)(2,1)S(1)}, u32[]{:S(2)}, u32[]{:S(2)}) collective-permute-start(bf16[128,1024]{1,0:T(8,128)(2,1)S(1)} %get-tuple-element.40), channel_id=1, source_target_pairs={{0,2},{2,0},{4,6},{6,4},{8,10},{10,8},{12,14},{14,12},{16,18},{18,... | collective-permute-start | bytes 786440 | tf_op jit(solution)/shard_map/ppermute | solution.py:320
  55.9 1.2 %collective-permute-done.15.theirs = bf16[128,1024]{1,0:T(8,128)(2,1)S(1)} collective-permute-done((bf16[128,1024]{1,0:T(8,128)(2,1)S(1)}, bf16[128,1024]{1,0:T(8,128)(2,1)S(1)}, u32[]{:S(2)}, u32[]{:S(2)}) %collective-permute-start.15) | collective-permute-done | bytes 262176 | tf_op jit(solution)/shard_map/ppermute | solution.py:320
  57.1 1.4 %shard_map.52 = bf16[128,2048]{1,0:T(8,128)(2,1)} custom-call(s32[11]{0:T(128)S(1)} %stack.41.facts_ref, bf16[128,1024]{1,0:T(8,128)(2,1)S(1)} %get-tuple-element.39.mine, bf16[128,1024]{1,0:T(8,128)(2,1)S(1)} %collective-permute-done.15.theirs), custom_call_target="tpu_custom_call" | custom-call | tf_op jit(solution)/shard_map/pallas_call | solution.py:418
  (29 shorter events, 3.7 us)
Async XLA Ops:
  0.0 2.9 %collective-permute-start = (bf16[64,4096]{1,0:T(8,128)(2,1)}, bf16[64,4096]{1,0:T(8,128)(2,1)S(1)}, u32[]{:S(2)}, u32[]{:S(2)}) collective-permute-start(bf16[64,4096]{1,0:T(8,128)(2,1)} %refs_0_.1), channel_id=1, source_target_pairs={{0,2},{2,0},{4,6},{6,4},{8,10},{10,8},{12,14},{14,12},{16,18},{18,... | collective-permute-start | bytes 1572872 | tf_op jit(solution)/shard_map/ppermute | solution.py:320
  0.7 13.8 %collective-permute-start.1 = (bf16[64,4096]{1,0:T(8,128)(2,1)}, bf16[64,4096]{1,0:T(8,128)(2,1)S(1)}, u32[]{:S(2)}, u32[]{:S(2)}) collective-permute-start(bf16[64,4096]{1,0:T(8,128)(2,1)} %refs_0_.1), channel_id=1, source_target_pairs={{0,1},{1,0},{2,3},{3,2},{4,5},{5,4},{6,7},{7,6},{8,9},{9,8},{10,11... | collective-permute-start | bytes 1572872 | tf_op jit(solution)/shard_map/ppermute | solution.py:328
  8.4 6.7 %collective-permute-start.2 = (bf16[128,512]{1,0:T(8,128)(2,1)S(1)}, bf16[128,512]{1,0:T(8,128)(2,1)S(1)}, u32[]{:S(2)}, u32[]{:S(2)}) collective-permute-start(bf16[128,512]{1,0:T(8,128)(2,1)S(1)} %get-tuple-element.24.refs_1_), channel_id=1, source_target_pairs={{0,8},{2,10},{4,12},{6,14},{8,16},{10,18},{12,20},{14,22},{16,24},... | collective-permute-start | bytes 393224 | tf_op jit(solution)/shard_map/ppermute | solution.py:359
  9.7 8.5 %collective-permute-start.3 = (bf16[128,512]{1,0:T(8,128)(2,1)S(1)}, bf16[128,512]{1,0:T(8,128)(2,1)S(1)}, u32[]{:S(2)}, u32[]{:S(2)}) collective-permute-start(bf16[128,512]{1,0:T(8,128)(2,1)S(1)} %get-tuple-element.24.refs_1_), channel_id=1, source_target_pairs={{0,24},{2,26},{4,28},{6,30},{1,25},{3,27},{5,29},{7,31}} | collective-permute-start | bytes 393224 | tf_op jit(solution)/shard_map/ppermute | solution.py:359
  11.0 7.2 %collective-permute-start.4 = (bf16[128,512]{1,0:T(8,128)(2,1)S(1)}, bf16[128,512]{1,0:T(8,128)(2,1)S(1)}, u32[]{:S(2)}, u32[]{:S(2)}) collective-permute-start(bf16[128,512]{1,0:T(8,128)(2,1)S(1)} %get-tuple-element.24.refs_1_), channel_id=1, source_target_pairs={{0,4},{2,6},{8,12},{10,14},{16,20},{18,22},{24,28},{26,30},{1,5},{... | collective-permute-start | bytes 393224 | tf_op jit(solution)/shard_map/ppermute | solution.py:372
  18.2 5.8 %collective-permute-start.5 = (bf16[64,4096]{1,0:T(8,128)(2,1)S(1)}, bf16[64,4096]{1,0:T(8,128)(2,1)S(1)}, u32[]{:S(2)}, u32[]{:S(2)}) collective-permute-start(bf16[64,4096]{1,0:T(8,128)(2,1)S(1)} %collective-permute-done.1.refs_0_), channel_id=1, source_target_pairs={{0,2},{2,0},{4,6},{6,4},{8,10},{10,8},{12,14},{14,12},{16,18},{18,... | collective-permute-start | bytes 1572872 | tf_op jit(solution)/shard_map/ppermute | solution.py:320
  19.5 11.7 %collective-permute-start.7 = (bf16[128,512]{1,0:T(8,128)(2,1)S(1)}, bf16[128,512]{1,0:T(8,128)(2,1)S(1)}, u32[]{:S(2)}, u32[]{:S(2)}) collective-permute-start(bf16[128,512]{1,0:T(8,128)(2,1)S(1)} %get-tuple-element.24.refs_1_), channel_id=1, source_target_pairs={{0,16},{2,18},{4,20},{6,22},{8,24},{10,26},{12,28},{14,30},{1,17},... | collective-permute-start | bytes 393224 | tf_op jit(solution)/shard_map/ppermute | solution.py:359
  20.8 15.3 %collective-permute-start.8 = (bf16[256,512]{1,0:T(8,128)(2,1)S(1)}, bf16[256,512]{1,0:T(8,128)(2,1)S(1)}, u32[]{:S(2)}, u32[]{:S(2)}) collective-permute-start(bf16[256,512]{1,0:T(8,128)(2,1)S(1)} %pad_maximum_fusion), channel_id=1, source_target_pairs={{8,12},{10,14},{12,8},{14,10},{16,20},{18,22},{20,16},{22,18},{24,... | collective-permute-start | bytes 786440 | tf_op jit(solution)/shard_map/ppermute | solution.py:372
  24.8 8.3 %collective-permute-start.12 = (bf16[128,512]{1,0:T(8,128)(2,1)S(1)}, bf16[128,512]{1,0:T(8,128)(2,1)S(1)}, u32[]{:S(2)}, u32[]{:S(2)}) collective-permute-start(bf16[128,512]{1,0:T(8,128)(2,1)S(1)} %get-tuple-element.29.refs_2_), channel_id=1, source_target_pairs={{0,8},{2,10},{4,12},{6,14},{8,16},{10,18},{12,20},{14,22},{16,24},... | collective-permute-start | bytes 393224 | tf_op jit(solution)/shard_map/ppermute | solution.py:359
  26.1 16.7 %collective-permute-start.10 = (bf16[128,512]{1,0:T(8,128)(2,1)S(1)}, bf16[128,512]{1,0:T(8,128)(2,1)S(1)}, u32[]{:S(2)}, u32[]{:S(2)}) collective-permute-start(bf16[128,512]{1,0:T(8,128)(2,1)S(1)} %get-tuple-element.29.refs_2_), channel_id=1, source_target_pairs={{0,24},{2,26},{4,28},{6,30},{1,25},{3,27},{5,29},{7,31}} | collective-permute-start | bytes 393224 | tf_op jit(solution)/shard_map/ppermute | solution.py:359
  27.4 17.4 %collective-permute-start.6 = (bf16[128,512]{1,0:T(8,128)(2,1)S(1)}, bf16[128,512]{1,0:T(8,128)(2,1)S(1)}, u32[]{:S(2)}, u32[]{:S(2)}) collective-permute-start(bf16[128,512]{1,0:T(8,128)(2,1)S(1)} %get-tuple-element.29.refs_2_), channel_id=1, source_target_pairs={{0,16},{2,18},{4,20},{6,22},{8,24},{10,26},{12,28},{14,30},{1,17},... | collective-permute-start | bytes 393224 | tf_op jit(solution)/shard_map/ppermute | solution.py:359
  33.1 15.2 %collective-permute-start.14 = (bf16[256,512]{1,0:T(8,128)(2,1)S(1)}, bf16[256,512]{1,0:T(8,128)(2,1)S(1)}, u32[]{:S(2)}, u32[]{:S(2)}) collective-permute-start(bf16[256,512]{1,0:T(8,128)(2,1)S(1)} %pad_maximum_fusion.1), channel_id=1, source_target_pairs={{8,12},{10,14},{12,8},{14,10},{16,20},{18,22},{20,16},{22,18},{24,... | collective-permute-start | bytes 786440 | tf_op jit(solution)/shard_map/ppermute | solution.py:372
  36.2 12.2 %collective-permute-start.13 = (bf16[128,512]{1,0:T(8,128)(2,1)S(1)}, bf16[128,512]{1,0:T(8,128)(2,1)S(1)}, u32[]{:S(2)}, u32[]{:S(2)}) collective-permute-start(bf16[128,512]{1,0:T(8,128)(2,1)S(1)} %get-tuple-element.29.refs_2_), channel_id=1, source_target_pairs={{0,4},{2,6},{8,12},{10,14},{16,20},{18,22},{24,28},{26,30},{1,5},{... | collective-permute-start | bytes 393224 | tf_op jit(solution)/shard_map/ppermute | solution.py:372
  42.8 9.2 %collective-permute-start.11 = (bf16[128,512]{1,0:T(8,128)(2,1)S(1)}, bf16[128,512]{1,0:T(8,128)(2,1)S(1)}, u32[]{:S(2)}, u32[]{:S(2)}) collective-permute-start(bf16[128,512]{1,0:T(8,128)(2,1)S(1)} %collective-permute-done.10.refs_3_), channel_id=1, source_target_pairs={{24,28},{26,30},{28,24},{30,26},{25,29},{27,31},{29,25},{31,27}} | collective-permute-start | bytes 393224 | tf_op jit(solution)/shard_map/ppermute | solution.py:372
  44.8 7.4 %collective-permute-start.9 = (bf16[128,512]{1,0:T(8,128)(2,1)S(1)}, bf16[128,512]{1,0:T(8,128)(2,1)S(1)}, u32[]{:S(2)}, u32[]{:S(2)}) collective-permute-start(bf16[128,512]{1,0:T(8,128)(2,1)S(1)} %collective-permute-done.6.refs_2_), channel_id=1, source_target_pairs={{16,20},{18,22},{20,16},{22,18},{24,28},{26,30},{28,24},{30,26},{1... | collective-permute-start | bytes 393224 | tf_op jit(solution)/shard_map/ppermute | solution.py:372
  54.2 2.9 %collective-permute-start.15 = (bf16[128,1024]{1,0:T(8,128)(2,1)S(1)}, bf16[128,1024]{1,0:T(8,128)(2,1)S(1)}, u32[]{:S(2)}, u32[]{:S(2)}) collective-permute-start(bf16[128,1024]{1,0:T(8,128)(2,1)S(1)} %get-tuple-element.40), channel_id=1, source_target_pairs={{0,2},{2,0},{4,6},{6,4},{8,10},{10,8},{12,14},{14,12},{16,18},{18,... | collective-permute-start | bytes 786440 | tf_op jit(solution)/shard_map/ppermute | solution.py:320

commit v3 on v2

--- a/solution.py
+++ b/solution.py
@@ -34,53 +34,29 @@
     out_ref[:, width:] = product[:, width:].astype(jnp.bfloat16)
 
 
-def first_kernel(parts, chunks, facts_ref, *refs):
-    rows_in = refs[:parts]
-    key_w, value_w, query_w, cosine, sine = refs[parts : parts + 5]
-    out_ref, rows_ref, kv_ref, q_ref, kv_sem, q_sem, row_sem = refs[parts + 5 :]
-    model = key_w.shape[0]
-    depth = model // chunks
+def load_kernel(chunks, facts_ref, *refs):
+    rows_in, key_w, value_w, rows_ref, kv_ref, kv_sem, row_sem = refs
+    depth = key_w.shape[0] // chunks
     width = kv_ref.shape[1] // 2
-    wide = q_ref.shape[1]
-    half = facts_ref[HALF]
-    narrow_at = pl.multiple_of(half * width, width)
-    wide_at = pl.multiple_of(half * wide, wide)
-    count = rows_in[0].shape[0]
-    own = pltpu.make_async_copy(rows_in[0], rows_ref.at[pl.ds(0, count)], row_sem)
-    small, large = [], []
+    at = pl.multiple_of(facts_ref[HALF] * width, width)
+    copies = [pltpu.make_async_copy(rows_in, rows_ref, row_sem)]
     for i in range(chunks):
         cut = pl.ds(i * depth, depth)
         for j, source in enumerate((key_w, value_w)):
-            small.append(
+            copies.append(
                 pltpu.make_async_copy(
-                    source.at[cut, pl.ds(narrow_at, width)],
+                    source.at[cut, pl.ds(at, width)],
                     kv_ref.at[cut, pl.ds(j * width, width)],
                     kv_sem.at[i, j],
                 )
             )
-        large.append(
-            pltpu.make_async_copy(
-                query_w.at[cut, pl.ds(wide_at, wide)], q_ref.at[cut, :], q_sem.at[i]
-            )
-        )
-    for copy in [own] + small + large:
+    for copy in copies:
         copy.start()
-    for i in range(1, parts):
-        rows_ref[i * count : (i + 1) * count, :] = rows_in[i][...]
-    own.wait()
-    product = None
-    for i in range(chunks):
-        small[2 * i].wait()
-        small[2 * i + 1].wait()
-        cut = slice(i * depth, (i + 1) * depth)
-        term = jnp.dot(rows_ref[:, cut], kv_ref[cut, :], preferred_element_type=jnp.float32)
-        product = term if product is None else product + term
-    write_kv(product, cosine, sine, out_ref)
-    for copy in large:
+    for copy in copies:
         copy.wait()
 
 
-def later_kernel(parts, *refs):
+def kv_kernel(parts, *refs):
     rows_in = refs[:parts]
     weight, cosine, sine, out_ref, rows_ref = refs[parts:]
     at = 0
@@ -91,16 +67,19 @@
     write_kv(product, cosine, sine, out_ref)
 
 
-def query_kernel(parts, *refs):
+def query_kernel(parts, facts_ref, *refs):
     rows_in = refs[:parts]
-    weight, cosine, sine, out_ref = refs[parts:]
-    rows = jnp.concatenate([r[...] for r in rows_in], axis=0)
+    weight, cosine, sine, out_ref, rows_ref = refs[parts:]
     heads = out_ref.shape[0]
+    at = 0
+    for r in rows_in:
+        rows_ref[at : at + r.shape[0], :] = r[...]
+        at += r.shape[0]
     step = math.gcd(heads, 2)
+    base = facts_ref[HALF] * (heads * HD)
     for at in range(0, heads, step):
-        product = jnp.dot(
-            rows, weight[:, at * HD : (at + step) * HD], preferred_element_type=jnp.float32
-        )
+        cut = pl.ds(pl.multiple_of(base + at * HD, step * HD), step * HD)
+        product = jnp.dot(rows_ref[...], weight[:, cut], preferred_element_type=jnp.float32)
         for h in range(step):
             head = product[:, h * HD : (h + 1) * HD]
             out_ref[at + h] = turn(head, cosine[...], sine[...]).astype(jnp.bfloat16)
@@ -118,40 +97,31 @@
     return pltpu.CompilerParams(vmem_limit_bytes=megabytes * 1024 * 1024)
 
 
-def project_first(facts, blocks, key_weight, value_weight, query_weight, cosine, sine, kv_heads, heads):
-    rows = sum(b.shape[0] for b in blocks)
+def far(array):
+    return pltpu.with_memory_space_constraint(array, pltpu.HBM)
+
+
+def load(facts, activations, key_weight, value_weight, width):
     model = key_weight.shape[0]
-    width = kv_heads * HD
-    chunks = 4
-    far = lambda a: pltpu.with_memory_space_constraint(a, pltpu.HBM)
+    chunks = 2
     return pl.pallas_call(
-        functools.partial(first_kernel, len(blocks), chunks),
+        functools.partial(load_kernel, chunks),
         out_shape=[
-            jax.ShapeDtypeStruct((rows, 2 * width), jnp.bfloat16),
-            pltpu.VMEM((rows, model), jnp.bfloat16),
+            pltpu.VMEM(activations.shape, jnp.bfloat16),
             pltpu.VMEM((model, 2 * width), jnp.bfloat16),
-            pltpu.VMEM((model, heads * HD), jnp.bfloat16),
         ],
-        in_specs=[SMEM, FAR] + [VMEM] * (len(blocks) - 1) + [FAR] * 3 + [VMEM] * 2,
-        out_specs=[VMEM] * 4,
-        scratch_shapes=[
-            pltpu.SemaphoreType.DMA((chunks, 2)),
-            pltpu.SemaphoreType.DMA((chunks,)),
-            pltpu.SemaphoreType.DMA(()),
-        ],
+        in_specs=[SMEM] + [FAR] * 3,
+        out_specs=[VMEM] * 2,
+        scratch_shapes=[pltpu.SemaphoreType.DMA((chunks, 2)), pltpu.SemaphoreType.DMA(())],
         compiler_params=params(24),
-        cost_estimate=pl.CostEstimate(
-            flops=4 * rows * model * width,
-            bytes_accessed=2 * model * (heads * HD + 2 * width),
-            transcendentals=0,
-        ),
-    )(facts, far(blocks[0]), *blocks[1:], far(key_weight), far(value_weight), far(query_weight), cosine, sine)
-
-
-def project_later(blocks, weight, cosine, sine):
+        cost_estimate=pl.CostEstimate(flops=0, bytes_accessed=4 * model * width, transcendentals=0),
+    )(facts, far(activations), far(key_weight), far(value_weight))
+
+
+def project_kv(blocks, weight, cosine, sine):
     rows = sum(b.shape[0] for b in blocks)
     return pl.pallas_call(
-        functools.partial(later_kernel, len(blocks)),
+        functools.partial(kv_kernel, len(blocks)),
         out_shape=[
             jax.ShapeDtypeStruct((rows, weight.shape[1]), jnp.bfloat16),
             pltpu.VMEM((rows, weight.shape[0]), jnp.bfloat16),
@@ -165,18 +135,22 @@
     )(*blocks, close(weight), cosine, sine)
 
 
-def project_q(blocks, weight, cosine, sine, heads):
+def project_q(facts, blocks, weight, cosine, sine, heads):
     rows = sum(b.shape[0] for b in blocks)
+    model = weight.shape[0]
     return pl.pallas_call(
         functools.partial(query_kernel, len(blocks)),
         out_shape=jax.ShapeDtypeStruct((heads, rows, HD), jnp.bfloat16),
-        in_specs=[VMEM] * (len(blocks) + 3),
+        in_specs=[SMEM] + [VMEM] * len(blocks) + [VMEM] * 3,
         out_specs=VMEM,
+        scratch_shapes=[
+            pltpu.VMEM((rows, model), jnp.bfloat16),
+        ],
         compiler_params=params(24),
         cost_estimate=pl.CostEstimate(
-            flops=2 * rows * weight.size, bytes_accessed=2 * weight.size, transcendentals=0
+            flops=0, bytes_accessed=0, transcendentals=0
         ),
-    )(*[close(b) for b in blocks], close(weight), cosine, sine)
+    )(facts, *[close(b) for b in blocks], close(weight), cosine, sine)
 
 
 def attend_kernel(first, last, own_count, origins, kv_heads, pair, block_rows, facts_ref, *refs):
@@ -347,38 +321,38 @@
 
     hops = range(1, outer)
 
-    def upward(piece):
-        columns = {}
-        for hop in hops:
-            links = [
-                (device(o, i, c), device(o + hop, i, c))
-                for o in range(outer - hop)
-                for i in range(inner)
-                for c in range(pair)
-            ]
-            columns[hop] = lax.ppermute(piece, "ctx", links)
-        return columns
-
-    def aside(block, first, parts=(0,)):
+    def upward(piece, hop):
+        links = [
+            (device(o, i, c), device(o + hop, i, c))
+            for o in range(outer - hop)
+            for i in range(inner)
+            for c in range(pair)
+        ]
+        return lax.ppermute(piece, "ctx", links)
+
+    def aside(blocks, origins):
         moved = []
         for turn_by in range(1, inner):
             links = [
                 (device(o, i, c), device(o, (i + turn_by) % inner, c))
-                for o in range(first, outer)
+                for o in range(outer)
                 for i in range(inner)
                 for c in range(pair)
-                if first > 0 or i + turn_by < inner
+                if any(o >= hop if hop else i + turn_by < inner for hop in origins)
             ]
-            block_in = lax.ppermute(block, "ctx", links)
-            for part, hop in zip(jnp.split(block_in, len(parts)), parts):
-                moved.append((part, (hop, turn_by)))
+            block = blocks[0] if len(blocks) == 1 else jnp.concatenate(blocks, axis=0)
+            block = lax.ppermute(block, "ctx", links)
+            at = 0
+            for b, hop in zip(blocks, origins):
+                moved.append((block[at : at + b.shape[0]], (hop, turn_by)))
+                at += b.shape[0]
         return moved
 
     state = None
 
     def fold(own, pieces, last):
         nonlocal state
-        limit = max(1, (1024 - local_rows) // max([block.shape[0] for block, _ in pieces] + [1]))
+        limit = max(1, 1408 // max([block.shape[0] for block, _ in pieces] + [1]))
         for i in range(0, max(1, len(pieces)), limit):
             some = pieces[i : i + limit]
             state = attend(
@@ -386,31 +360,41 @@
                 state, last and i + limit >= len(pieces), kv_heads, pair, rows_here,
             )
 
-    held = both(blocks[:1])
+    own_rows, kv_weight = load(facts, activations, key_weight, value_weight, kv_heads * HD)
+    held = [own_rows] + both(blocks[:1])[1:]
     count = len(held) * rows_here
-    first, first_rows, kv_weight, q_weight = project_first(
-        facts, held, key_weight, value_weight, query_weight, cosine[:count], sine[:count], kv_heads, heads
-    )
-    columns = upward(first)
-    beside = aside(first, 0)
-    early = [hop for hop in hops if hop != 2]
-    gate = [columns[hop] for hop in early] + [b for b, _ in beside]
+    first, first_rows = project_kv(held, kv_weight, cosine[:count], sine[:count])
+    early = [hop for hop in hops if hop == 1]
+    columns = {hop: upward(first, hop) for hop in early}
+    beside = []
+    gate = [columns[hop] for hop in early[:1]]
     late = both([after(b, gate) for b in blocks[1:]])
-    second, second_rows = project_later(late, kv_weight, cosine[count:], sine[count:])
-    pieces = [(columns[hop], (hop, 0)) for hop in hops] + beside
+    second, second_rows = project_kv(late, kv_weight, cosine[count:], sine[count:])
+    middle = []
     if early:
-        pieces += aside(jnp.concatenate([columns[hop] for hop in early], axis=0), 1, early)
-    later = upward(second)
-    more = [(later[hop], (hop, 0)) for hop in hops] + aside(second, 0)
-    queries = project_q([first_rows, second_rows], q_weight, cosine, sine, heads)
-    if early:
-        block, parts = later[1], [1]
-        if outer > 2:
-            block, parts = jnp.concatenate([later[1], columns[2]], axis=0), [1, 2]
-        more += aside(after(block, [queries]), 1, parts)
-    fold([first, second], pieces, False)
-    last = [m for hop in hops if hop > 1 for m in aside(after(later[hop], state[:1]), hop, [hop])]
-    fold([], more, not last)
+        chained = [columns[1]] if outer > 2 else []
+        block = upward(jnp.concatenate(chained + [second], axis=0), 1)
+        middle = [(block[first.shape[0] * len(chained) :], (1, 0))]
+        if chained:
+            middle.append((block[: first.shape[0]], (2, 0)))
+    direct = []
+    for hop in hops:
+        if hop == 2:
+            direct.append((upward(second, hop), (hop, 0)))
+        elif hop > 2:
+            both_waves = upward(jnp.concatenate([first, second], axis=0), hop)
+            direct += [(both_waves[: first.shape[0]], (hop, 0)), (both_waves[first.shape[0] :], (hop, 0))]
+    forwarded = aside([first] + [columns[hop] for hop in early[:1]] + [second], [0] + early[:1] + [0])
+    queries = project_q(facts, [first_rows, second_rows], query_weight, cosine, sine, heads)
+    again, last = [], []
+    if middle:
+        again = aside([after(b, [queries]) for b, _ in middle], [o[0] for _, o in middle])
+    direct += [(columns[hop], (hop, 0)) for hop in early[1:]]
+    if direct:
+        last = aside([after(b, [m for m, _ in forwarded[:1]]) for b, _ in direct], [o[0] for _, o in direct])
+    straight = [(columns[hop], (hop, 0)) for hop in early[:1]] + beside
+    fold([first, second], straight + forwarded, False)
+    fold([], middle + direct + again, not last)
     if last:
         fold([], last, True)
     if pair == 1:

time: 58.8 us -> 57 us (0.969)
  starting transfers between devices: 29.5 us -> 19.2 us
  waiting for transfers between devices: 7.25 us -> 16.4 us
  Pallas kernels: 20.2 us -> 19.6 us
    ppermute x12 -> x7, starting transfers between devices: 24.8 us -> 14 us  [the longest x3 8.61 us: aside(): block = lax.ppermute(block, 'ctx', links)]
    ppermute x1, waiting for transfers between devices: 0.28 us -> 4.31 us  [local(): blocks.append(lax.ppermute(activations, 'tp', links))]
    ppermute x12 -> x7, waiting for transfers between devices: 5.79 us -> 9.4 us  [the longest x4 9.25 us: upward(): return lax.ppermute(piece, 'ctx', links)]
    pallas_call x2 -> x3, Pallas kernels: 6.3 us -> 4.74 us  [the longest x1 3.15 us: load(): pl.pallas_call(functools.partial(load_kernel, chunks), out_shape=[pltpu.V...]
    ppermute x3, waiting for transfers between devices: 1.17 us -> 2.7 us  [swap(): lax.ppermute(block, 'ctx', [(i, i ^ 1) for i in range(context_count)])]
    pallas_call x1, Pallas kernels: 2.48 us -> 3.11 us  [project_q(): pl.pallas_call(functools.partial(query_kernel, len(blocks)), out_shape=ja...]
  transfers between devices with their start and end apart: 16 -> 11, of which waited for: 6 -> 7; matrix products, arithmetic and copies ran while one was open for 2% -> 2% of each run, Pallas kernels for 29% -> 26%
where the time goes in v3:
time: 57 us; the launch traced here: 56.8 us
  Pallas kernels  19.6 us (34%)
  starting transfers between devices  19.2 us (34%)
  waiting for transfers between devices  16.4 us (29%)
  other arithmetic  1.14 us (2%)
    pallas_call x3, Pallas kernels, attend(): pl.pallas_call(functools.partial(attend_kernel, first, last, len(own), or...  10.4 us
    ppermute x4, waiting for transfers between devices, upward(): return lax.ppermute(piece, 'ctx', links)  9.25 us
    ppermute x3, starting transfers between devices, aside(): block = lax.ppermute(block, 'ctx', links)  8.61 us
    ppermute x4, starting transfers between devices, upward(): return lax.ppermute(piece, 'ctx', links)  5.43 us
    ppermute x1, waiting for transfers between devices, local(): blocks.append(lax.ppermute(activations, 'tp', links))  4.31 us
    ppermute x3, starting transfers between devices, swap(): lax.ppermute(block, 'ctx', [(i, i ^ 1) for i in range(context_count)])  3.93 us
    pallas_call x1, Pallas kernels, load(): pl.pallas_call(functools.partial(load_kernel, chunks), out_shape=[pltpu.V...  3.15 us
    pallas_call x1, Pallas kernels, project_q(): pl.pallas_call(functools.partial(query_kernel, len(blocks)), out_shape=ja...  3.11 us
  transfers between devices with their start and end apart: 11, of which 7 were waited for; matrix products, arithmetic and copies ran while one was open for 2% of the time, Pallas kernels for 26%

profile of v3, /device:TPU:25, one launch (start us, length us, event | category | flops | bytes accessed | tf_op | source)
XLA Modules:
  0.0 56.8 jit_solution(2723837081920523544)
XLA Ops:
  0.0 1.2 %collective-permute-start.1 = (bf16[64,4096]{1,0:T(8,128)(2,1)}, bf16[64,4096]{1,0:T(8,128)(2,1)S(1)}, u32[]{:S(2)}, u32[]{:S(2)}) collective-permute-start(bf16[64,4096]{1,0:T(8,128)(2,1)} %refs_0_.1), channel_id=1, source_target_pairs={{0,1},{1,0},{2,3},{3,2},{4,5},{5,4},{6,7},{7,6},{8,9},{9,8},{10,11... | collective-permute-start | bytes 1572872 | tf_op jit(solution)/shard_map/ppermute | solution.py:302
  1.2 1.0 %collective-permute-start = (bf16[64,4096]{1,0:T(8,128)(2,1)}, bf16[64,4096]{1,0:T(8,128)(2,1)S(1)}, u32[]{:S(2)}, u32[]{:S(2)}) collective-permute-start(bf16[64,4096]{1,0:T(8,128)(2,1)} %refs_0_.1), channel_id=1, source_target_pairs={{0,2},{2,0},{4,6},{6,4},{8,10},{10,8},{12,14},{14,12},{16,18},{18,... | collective-permute-start | bytes 1572872 | tf_op jit(solution)/shard_map/ppermute | solution.py:294
  2.9 3.1 %shard_map.46 = (bf16[64,4096]{1,0:T(8,128)(2,1)S(1)}, bf16[4096,512]{1,0:T(8,128)(2,1)S(1)}) custom-call(s32[11]{0:T(128)S(1)} %stack.41.facts_ref, bf16[64,4096]{1,0:T(8,128)(2,1)} %refs_0_.1, bf16[4096,512]{1,0:T(8,128)(2,1)} %refs_1_.1, bf16[4096,512]{1,0:T(8,128)(2,1)} %refs_2_.2), custom_call_target="tpu_custom_call" | custom-call | bytes 4194304 | tf_op jit(solution)/shard_map/pallas_call | solution.py:107
  6.3 0.8 %shard_map.47 = (bf16[128,512]{1,0:T(8,128)(2,1)S(1)}, bf16[128,4096]{1,0:T(8,128)(2,1)S(1)}) custom-call(bf16[64,4096]{1,0:T(8,128)(2,1)S(1)} %get-tuple-element.25.refs_0_, bf16[64,4096]{1,0:T(8,128)(2,1)S(1)} %collective-permute-done.refs_1_, bf16[4096,512]{1,0:T(8,128)(2,1)S(1)} %get-tuple-element.26.refs_2_, f32[128,128]{1,0:T(8,128)S(1)} %get-tuple-element.62.refs_3_, ...), custom_call_target="tpu_custom_call" | custom-call | flops 536870912 | bytes 4194304 | tf_op jit(solution)/shard_map/pallas_call | solution.py:123
  7.1 1.6 %collective-permute-start.2 = (bf16[128,512]{1,0:T(8,128)(2,1)S(1)}, bf16[128,512]{1,0:T(8,128)(2,1)S(1)}, u32[]{:S(2)}, u32[]{:S(2)}) collective-permute-start(bf16[128,512]{1,0:T(8,128)(2,1)S(1)} %get-tuple-element.28.refs_1_), channel_id=1, source_target_pairs={{0,8},{2,10},{4,12},{6,14},{8,16},{10,18},{12,20},{14,22},{16,24},... | collective-permute-start | bytes 393224 | tf_op jit(solution)/shard_map/ppermute | solution.py:331
  8.7 4.3 %collective-permute-done.1.refs_0_ = bf16[64,4096]{1,0:T(8,128)(2,1)S(1)} collective-permute-done((bf16[64,4096]{1,0:T(8,128)(2,1)}, bf16[64,4096]{1,0:T(8,128)(2,1)S(1)}, u32[]{:S(2)}, u32[]{:S(2)}) %collective-permute-start.1) | collective-permute-done | bytes 524320 | tf_op jit(solution)/shard_map/ppermute | solution.py:302
  13.0 1.4 %collective-permute-done.2.refs_3_ = bf16[128,512]{1,0:T(8,128)(2,1)S(1)} collective-permute-done((bf16[128,512]{1,0:T(8,128)(2,1)S(1)}, bf16[128,512]{1,0:T(8,128)(2,1)S(1)}, u32[]{:S(2)}, u32[]{:S(2)}) %collective-permute-start.2) | collective-permute-done | bytes 131104 | tf_op jit(solution)/shard_map/ppermute | solution.py:331
  14.4 0.8 %collective-permute-start.3 = (bf16[64,4096]{1,0:T(8,128)(2,1)S(1)}, bf16[64,4096]{1,0:T(8,128)(2,1)S(1)}, u32[]{:S(2)}, u32[]{:S(2)}) collective-permute-start(bf16[64,4096]{1,0:T(8,128)(2,1)S(1)} %collective-permute-done.1.refs_0_), channel_id=1, source_target_pairs={{0,2},{2,0},{4,6},{6,4},{8,10},{10,8},{12,14},{14,12},{16,18},{18,... | collective-permute-start | bytes 1572872 | tf_op jit(solution)/shard_map/ppermute | solution.py:294
  15.2 1.5 %collective-permute-done.3.refs_1_ = bf16[64,4096]{1,0:T(8,128)(2,1)S(1)} collective-permute-done((bf16[64,4096]{1,0:T(8,128)(2,1)S(1)}, bf16[64,4096]{1,0:T(8,128)(2,1)S(1)}, u32[]{:S(2)}, u32[]{:S(2)}) %collective-permute-start.3) | collective-permute-done | bytes 524320 | tf_op jit(solution)/shard_map/ppermute | solution.py:294
  17.6 1.3 %collective-permute-start.8 = (bf16[256,512]{1,0:T(8,128)(2,1)S(1)}, bf16[256,512]{1,0:T(8,128)(2,1)S(1)}, u32[]{:S(2)}, u32[]{:S(2)}) collective-permute-start(bf16[256,512]{1,0:T(8,128)(2,1)S(1)} %get-tuple-element.59), channel_id=1, source_target_pairs={{0,8},{2,10},{4,12},{6,14},{8,16},{10,18},{12,20},{14,22},{16,24},... | collective-permute-start | bytes 786440 | tf_op jit(solution)/shard_map/ppermute | solution.py:331
  19.1 1.3 %collective-permute-start.4 = (bf16[128,512]{1,0:T(8,128)(2,1)S(1)}, bf16[128,512]{1,0:T(8,128)(2,1)S(1)}, u32[]{:S(2)}, u32[]{:S(2)}) collective-permute-start(bf16[128,512]{1,0:T(8,128)(2,1)S(1)} %get-tuple-element.31.refs_2_), channel_id=1, source_target_pairs={{0,16},{2,18},{4,20},{6,22},{8,24},{10,26},{12,28},{14,30},{1,17},... | collective-permute-start | bytes 393224 | tf_op jit(solution)/shard_map/ppermute | solution.py:331
  20.4 3.1 %collective-permute-start.5 = (bf16[384,512]{1,0:T(8,128)(2,1)S(1)}, bf16[384,512]{1,0:T(8,128)(2,1)S(1)}, u32[]{:S(2)}, u32[]{:S(2)}) collective-permute-start(bf16[384,512]{1,0:T(8,128)(2,1)S(1)} %pad_maximum_fusion), channel_id=1, source_target_pairs={{0,4},{2,6},{8,12},{10,14},{12,8},{14,10},{16,20},{18,22},{20,16},... | collective-permute-start | bytes 1179656 | tf_op jit(solution)/shard_map/ppermute | solution.py:344
  23.6 1.3 %collective-permute-start.6 = (bf16[256,512]{1,0:T(8,128)(2,1)S(1)}, bf16[256,512]{1,0:T(8,128)(2,1)S(1)}, u32[]{:S(2)}, u32[]{:S(2)}) collective-permute-start(bf16[256,512]{1,0:T(8,128)(2,1)S(1)} %get-tuple-element.60), channel_id=1, source_target_pairs={{0,24},{2,26},{4,28},{6,30},{1,25},{3,27},{5,29},{7,31}} | collective-permute-start | bytes 786440 | tf_op jit(solution)/shard_map/ppermute | solution.py:331
  24.9 3.1 %shard_map.49.refs_0_ = bf16[8,256,128]{2,1,0:T(8,128)(2,1)S(1)} custom-call(s32[11]{0:T(128)S(1)} %stack.41.facts_ref, bf16[128,4096]{1,0:T(8,128)(2,1)S(1)} %get-tuple-element.27.refs_0_, bf16[128,4096]{1,0:T(8,128)(2,1)S(1)} %get-tuple-element.30.refs_1_, bf16[4096,2048]{1,0:T(8,128)(2,1)S(1)} %copy-done, f32[256,128]{1,0:T(8,128)S(1)} %pad_maximum_fusion.5.refs_3_, ...), custom_call_target="tpu_custom_call" | custom-call | tf_op jit(solution)/shard_map/pallas_call | solution.py:141
  28.1 2.1 %collective-permute-start.9 = (bf16[256,512]{1,0:T(8,128)(2,1)S(1)}, bf16[256,512]{1,0:T(8,128)(2,1)S(1)}, u32[]{:S(2)}, u32[]{:S(2)}) collective-permute-start(bf16[256,512]{1,0:T(8,128)(2,1)S(1)} %pad_maximum_fusion.4), channel_id=1, source_target_pairs={{8,12},{10,14},{12,8},{14,10},{16,20},{18,22},{20,16},{22,18},{24,... | collective-permute-start | bytes 786440 | tf_op jit(solution)/shard_map/ppermute | solution.py:344
  30.2 4.9 %collective-permute-done.6 = bf16[256,512]{1,0:T(8,128)(2,1)S(1)} collective-permute-done((bf16[256,512]{1,0:T(8,128)(2,1)S(1)}, bf16[256,512]{1,0:T(8,128)(2,1)S(1)}, u32[]{:S(2)}, u32[]{:S(2)}) %collective-permute-start.6) | collective-permute-done | bytes 262176 | tf_op jit(solution)/shard_map/ppermute | solution.py:331
  35.1 3.0 %collective-permute-done.4.refs_3_ = bf16[128,512]{1,0:T(8,128)(2,1)S(1)} collective-permute-done((bf16[128,512]{1,0:T(8,128)(2,1)S(1)}, bf16[128,512]{1,0:T(8,128)(2,1)S(1)}, u32[]{:S(2)}, u32[]{:S(2)}) %collective-permute-start.4) | collective-permute-done | bytes 131104 | tf_op jit(solution)/shard_map/ppermute | solution.py:331
  38.1 3.3 %collective-permute-start.7 = (bf16[384,512]{1,0:T(8,128)(2,1)S(1)}, bf16[384,512]{1,0:T(8,128)(2,1)S(1)}, u32[]{:S(2)}, u32[]{:S(2)}) collective-permute-start(bf16[384,512]{1,0:T(8,128)(2,1)S(1)} %pad_maximum_fusion.1), channel_id=1, source_target_pairs={{16,20},{18,22},{20,16},{22,18},{24,28},{26,30},{28,24},{30,26},{1... | collective-permute-start | bytes 1179656 | tf_op jit(solution)/shard_map/ppermute | solution.py:344
  41.5 3.4 %shard_map.50 = (f32[8,256,128]{2,1,0:T(8,128)S(1)}, f32[8,256,128]{2,1,0:T(8,128)S(1)}, f32[8,256,128]{2,1,0:T(8,128)S(1)}) custom-call(s32[11]{0:T(128)S(1)} %stack.41.facts_ref, bf16[8,256,128]{2,1,0:T(8,128)(2,1)S(1)} %shard_map.49.refs_0_, bf16[128,512]{1,0:T(8,128)(2,1)S(1)} %get-tuple-element.28.refs_1_, ...), custom_call_target="tpu_custom_call" | custom-call | flops 805306368 | bytes 1048576 | tf_op jit(solution)/shard_map/pallas_call | solution.py:256
  44.9 4.4 %shard_map.51 = (f32[8,256,128]{2,1,0:T(8,128)S(1)}, f32[8,256,128]{2,1,0:T(8,128)S(1)}, f32[8,256,128]{2,1,0:T(8,128)S(1)}) custom-call(s32[11]{0:T(128)S(1)} %stack.41.facts_ref, bf16[8,256,128]{2,1,0:T(8,128)(2,1)S(1)} %shard_map.49.refs_0_, bf16[128,512]{1,0:T(8,128)(2,1)S(1)} %get-tuple-element.35.refs_1_, ...), custom_call_target="tpu_custom_call" | custom-call | flops 939524096 | bytes 1048576 | tf_op jit(solution)/shard_map/pallas_call | solution.py:256
  49.5 2.6 %shard_map.52 = (bf16[128,1024]{1,0:T(8,128)(2,1)S(1)}, bf16[128,1024]{1,0:T(8,128)(2,1)S(1)}) custom-call(s32[11]{0:T(128)S(1)} %stack.41.facts_ref, bf16[8,256,128]{2,1,0:T(8,128)(2,1)S(1)} %shard_map.49.refs_0_, bf16[128,512]{1,0:T(8,128)(2,1)S(1)} %get-tuple-element.50.refs_1_, bf16[128,512]{1,0:T(8,128)(2,1)S(1)} %get-tuple-element.49.refs_2_, ...), custom_call_target="tpu_custom_call" | custom-call | flops 402653184 | bytes 1048576 | tf_op jit(solution)/shard_map/pallas_call | solution.py:256
  52.1 2.2 %collective-permute-start.10 = (bf16[128,1024]{1,0:T(8,128)(2,1)S(1)}, bf16[128,1024]{1,0:T(8,128)(2,1)S(1)}, u32[]{:S(2)}, u32[]{:S(2)}) collective-permute-start(bf16[128,1024]{1,0:T(8,128)(2,1)S(1)} %get-tuple-element.44), channel_id=1, source_target_pairs={{0,2},{2,0},{4,6},{6,4},{8,10},{10,8},{12,14},{14,12},{16,18},{18,... | collective-permute-start | bytes 786440 | tf_op jit(solution)/shard_map/ppermute | solution.py:294
  54.2 1.2 %collective-permute-done.10.theirs = bf16[128,1024]{1,0:T(8,128)(2,1)S(1)} collective-permute-done((bf16[128,1024]{1,0:T(8,128)(2,1)S(1)}, bf16[128,1024]{1,0:T(8,128)(2,1)S(1)}, u32[]{:S(2)}, u32[]{:S(2)}) %collective-permute-start.10) | collective-permute-done | bytes 262176 | tf_op jit(solution)/shard_map/ppermute | solution.py:294
  55.4 1.4 %shard_map.53 = bf16[128,2048]{1,0:T(8,128)(2,1)} custom-call(s32[11]{0:T(128)S(1)} %stack.41.facts_ref, bf16[128,1024]{1,0:T(8,128)(2,1)S(1)} %get-tuple-element.43.mine, bf16[128,1024]{1,0:T(8,128)(2,1)S(1)} %collective-permute-done.10.theirs), custom_call_target="tpu_custom_call" | custom-call | tf_op jit(solution)/shard_map/pallas_call | solution.py:402
  (27 shorter events, 2.3 us)
Async XLA Ops:
  0.0 13.0 %collective-permute-start.1 = (bf16[64,4096]{1,0:T(8,128)(2,1)}, bf16[64,4096]{1,0:T(8,128)(2,1)S(1)}, u32[]{:S(2)}, u32[]{:S(2)}) collective-permute-start(bf16[64,4096]{1,0:T(8,128)(2,1)} %refs_0_.1), channel_id=1, source_target_pairs={{0,1},{1,0},{2,3},{3,2},{4,5},{5,4},{6,7},{7,6},{8,9},{9,8},{10,11... | collective-permute-start | bytes 1572872 | tf_op jit(solution)/shard_map/ppermute | solution.py:302
  1.2 5.1 %collective-permute-start = (bf16[64,4096]{1,0:T(8,128)(2,1)}, bf16[64,4096]{1,0:T(8,128)(2,1)S(1)}, u32[]{:S(2)}, u32[]{:S(2)}) collective-permute-start(bf16[64,4096]{1,0:T(8,128)(2,1)} %refs_0_.1), channel_id=1, source_target_pairs={{0,2},{2,0},{4,6},{6,4},{8,10},{10,8},{12,14},{14,12},{16,18},{18,... | collective-permute-start | bytes 1572872 | tf_op jit(solution)/shard_map/ppermute | solution.py:294
  2.9 22.0 %copy-start = (bf16[4096,2048]{1,0:T(8,128)(2,1)S(1)}, bf16[4096,2048]{1,0:T(8,128)(2,1)}, u32[]{:S(2)}) copy-start(bf16[4096,2048]{1,0:T(8,128)(2,1)} %refs_2_.3) | copy-start | bytes 50331652
  7.1 7.3 %collective-permute-start.2 = (bf16[128,512]{1,0:T(8,128)(2,1)S(1)}, bf16[128,512]{1,0:T(8,128)(2,1)S(1)}, u32[]{:S(2)}, u32[]{:S(2)}) collective-permute-start(bf16[128,512]{1,0:T(8,128)(2,1)S(1)} %get-tuple-element.28.refs_1_), channel_id=1, source_target_pairs={{0,8},{2,10},{4,12},{6,14},{8,16},{10,18},{12,20},{14,22},{16,24},... | collective-permute-start | bytes 393224 | tf_op jit(solution)/shard_map/ppermute | solution.py:331
  14.4 2.3 %collective-permute-start.3 = (bf16[64,4096]{1,0:T(8,128)(2,1)S(1)}, bf16[64,4096]{1,0:T(8,128)(2,1)S(1)}, u32[]{:S(2)}, u32[]{:S(2)}) collective-permute-start(bf16[64,4096]{1,0:T(8,128)(2,1)S(1)} %collective-permute-done.1.refs_0_), channel_id=1, source_target_pairs={{0,2},{2,0},{4,6},{6,4},{8,10},{10,8},{12,14},{14,12},{16,18},{18,... | collective-permute-start | bytes 1572872 | tf_op jit(solution)/shard_map/ppermute | solution.py:294
  17.6 10.4 %collective-permute-start.8 = (bf16[256,512]{1,0:T(8,128)(2,1)S(1)}, bf16[256,512]{1,0:T(8,128)(2,1)S(1)}, u32[]{:S(2)}, u32[]{:S(2)}) collective-permute-start(bf16[256,512]{1,0:T(8,128)(2,1)S(1)} %get-tuple-element.59), channel_id=1, source_target_pairs={{0,8},{2,10},{4,12},{6,14},{8,16},{10,18},{12,20},{14,22},{16,24},... | collective-permute-start | bytes 786440 | tf_op jit(solution)/shard_map/ppermute | solution.py:331
  19.1 19.0 %collective-permute-start.4 = (bf16[128,512]{1,0:T(8,128)(2,1)S(1)}, bf16[128,512]{1,0:T(8,128)(2,1)S(1)}, u32[]{:S(2)}, u32[]{:S(2)}) collective-permute-start(bf16[128,512]{1,0:T(8,128)(2,1)S(1)} %get-tuple-element.31.refs_2_), channel_id=1, source_target_pairs={{0,16},{2,18},{4,20},{6,22},{8,24},{10,26},{12,28},{14,30},{1,17},... | collective-permute-start | bytes 393224 | tf_op jit(solution)/shard_map/ppermute | solution.py:331
  20.4 14.7 %collective-permute-start.5 = (bf16[384,512]{1,0:T(8,128)(2,1)S(1)}, bf16[384,512]{1,0:T(8,128)(2,1)S(1)}, u32[]{:S(2)}, u32[]{:S(2)}) collective-permute-start(bf16[384,512]{1,0:T(8,128)(2,1)S(1)} %pad_maximum_fusion), channel_id=1, source_target_pairs={{0,4},{2,6},{8,12},{10,14},{12,8},{14,10},{16,20},{18,22},{20,16},... | collective-permute-start | bytes 1179656 | tf_op jit(solution)/shard_map/ppermute | solution.py:344
  23.6 11.5 %collective-permute-start.6 = (bf16[256,512]{1,0:T(8,128)(2,1)S(1)}, bf16[256,512]{1,0:T(8,128)(2,1)S(1)}, u32[]{:S(2)}, u32[]{:S(2)}) collective-permute-start(bf16[256,512]{1,0:T(8,128)(2,1)S(1)} %get-tuple-element.60), channel_id=1, source_target_pairs={{0,24},{2,26},{4,28},{6,30},{1,25},{3,27},{5,29},{7,31}} | collective-permute-start | bytes 786440 | tf_op jit(solution)/shard_map/ppermute | solution.py:331
  28.1 16.8 %collective-permute-start.9 = (bf16[256,512]{1,0:T(8,128)(2,1)S(1)}, bf16[256,512]{1,0:T(8,128)(2,1)S(1)}, u32[]{:S(2)}, u32[]{:S(2)}) collective-permute-start(bf16[256,512]{1,0:T(8,128)(2,1)S(1)} %pad_maximum_fusion.4), channel_id=1, source_target_pairs={{8,12},{10,14},{12,8},{14,10},{16,20},{18,22},{20,16},{22,18},{24,... | collective-permute-start | bytes 786440 | tf_op jit(solution)/shard_map/ppermute | solution.py:344
  38.1 11.3 %collective-permute-start.7 = (bf16[384,512]{1,0:T(8,128)(2,1)S(1)}, bf16[384,512]{1,0:T(8,128)(2,1)S(1)}, u32[]{:S(2)}, u32[]{:S(2)}) collective-permute-start(bf16[384,512]{1,0:T(8,128)(2,1)S(1)} %pad_maximum_fusion.1), channel_id=1, source_target_pairs={{16,20},{18,22},{20,16},{22,18},{24,28},{26,30},{28,24},{30,26},{1... | collective-permute-start | bytes 1179656 | tf_op jit(solution)/shard_map/ppermute | solution.py:344
  52.1 3.4 %collective-permute-start.10 = (bf16[128,1024]{1,0:T(8,128)(2,1)S(1)}, bf16[128,1024]{1,0:T(8,128)(2,1)S(1)}, u32[]{:S(2)}, u32[]{:S(2)}) collective-permute-start(bf16[128,1024]{1,0:T(8,128)(2,1)S(1)} %get-tuple-element.44), channel_id=1, source_target_pairs={{0,2},{2,0},{4,6},{6,4},{8,10},{10,8},{12,14},{14,12},{16,18},{18,... | collective-permute-start | bytes 786440 | tf_op jit(solution)/shard_map/ppermute | solution.py:294

commit v4 on v3

--- a/solution.py
+++ b/solution.py
@@ -386,15 +386,15 @@
             direct += [(both_waves[: first.shape[0]], (hop, 0)), (both_waves[first.shape[0] :], (hop, 0))]
     forwarded = aside([first] + [columns[hop] for hop in early[:1]] + [second], [0] + early[:1] + [0])
     queries = project_q(facts, [first_rows, second_rows], query_weight, cosine, sine, heads)
+    straight = [(columns[hop], (hop, 0)) for hop in early]
+    fold([first, second], straight, not middle)
     again, last = [], []
     if middle:
-        again = aside([after(b, [queries]) for b, _ in middle], [o[0] for _, o in middle])
-    direct += [(columns[hop], (hop, 0)) for hop in early[1:]]
+        again = aside([after(b, state[:1]) for b, _ in middle], [o[0] for _, o in middle])
     if direct:
         last = aside([after(b, [m for m, _ in forwarded[:1]]) for b, _ in direct], [o[0] for _, o in direct])
-    straight = [(columns[hop], (hop, 0)) for hop in early[:1]] + beside
-    fold([first, second], straight + forwarded, False)
-    fold([], middle + direct + again, not last)
+    if middle:
+        fold([], forwarded + middle + direct + again, not last)
     if last:
         fold([], last, True)
     if pair == 1:

time: 57 us -> 57.1 us (level)
  waiting for transfers between devices: 16.4 us -> 17.1 us
    ppermute x4, waiting for transfers between devices: 9.25 us -> 5.89 us  [upward(): return lax.ppermute(piece, 'ctx', links)]
    ppermute x3, waiting for transfers between devices: 0.15 us -> 2.6 us  [aside(): block = lax.ppermute(block, 'ctx', links)]
    ppermute x1, waiting for transfers between devices: 4.31 us -> 6.05 us  [local(): blocks.append(lax.ppermute(activations, 'tp', links))]
  transfers between devices with their start and end apart: 11 -> 11, of which waited for: 7 -> 6; matrix products, arithmetic and copies ran while one was open for 2% -> 2% of each run, Pallas kernels for 26% -> 25%
where the time goes in v4:
time: 57.1 us; the launch traced here: 56.8 us
  Pallas kernels  19.1 us (33%)
  starting transfers between devices  18.9 us (33%)
  waiting for transfers between devices  17.1 us (30%)
  other arithmetic  1.14 us (2%)
    pallas_call x3, Pallas kernels, attend(): pl.pallas_call(functools.partial(attend_kernel, first, last, len(own), or...  9.94 us
    ppermute x3, starting transfers between devices, aside(): block = lax.ppermute(block, 'ctx', links)  8.61 us
    ppermute x1, waiting for transfers between devices, local(): blocks.append(lax.ppermute(activations, 'tp', links))  6.05 us
    ppermute x4, waiting for transfers between devices, upward(): return lax.ppermute(piece, 'ctx', links)  5.89 us
    ppermute x4, starting transfers between devices, upward(): return lax.ppermute(piece, 'ctx', links)  5.43 us
    ppermute x3, starting transfers between devices, swap(): lax.ppermute(block, 'ctx', [(i, i ^ 1) for i in range(context_count)])  3.65 us
    pallas_call x1, Pallas kernels, load(): pl.pallas_call(functools.partial(load_kernel, chunks), out_shape=[pltpu.V...  3.15 us
    pallas_call x1, Pallas kernels, project_q(): pl.pallas_call(functools.partial(query_kernel, len(blocks)), out_shape=ja...  3.11 us
  transfers between devices with their start and end apart: 11, of which 6 were waited for; matrix products, arithmetic and copies ran while one was open for 2% of the time, Pallas kernels for 25%

profile of v4, /device:TPU:25, one launch (start us, length us, event | category | flops | bytes accessed | tf_op | source)
XLA Modules:
  0.0 56.8 jit_solution(10913445529038221931)
XLA Ops:
  0.7 1.2 %collective-permute-start.1 = (bf16[64,4096]{1,0:T(8,128)(2,1)}, bf16[64,4096]{1,0:T(8,128)(2,1)S(1)}, u32[]{:S(2)}, u32[]{:S(2)}) collective-permute-start(bf16[64,4096]{1,0:T(8,128)(2,1)} %refs_0_.1), channel_id=1, source_target_pairs={{0,1},{1,0},{2,3},{3,2},{4,5},{5,4},{6,7},{7,6},{8,9},{9,8},{10,11... | collective-permute-start | bytes 1572872 | tf_op jit(solution)/shard_map/ppermute | solution.py:302
  2.7 3.1 %shard_map.46 = (bf16[64,4096]{1,0:T(8,128)(2,1)S(1)}, bf16[4096,512]{1,0:T(8,128)(2,1)S(1)}) custom-call(s32[11]{0:T(128)S(1)} %stack.41.facts_ref, bf16[64,4096]{1,0:T(8,128)(2,1)} %refs_0_.1, bf16[4096,512]{1,0:T(8,128)(2,1)} %refs_1_.1, bf16[4096,512]{1,0:T(8,128)(2,1)} %refs_2_.2), custom_call_target="tpu_custom_call" | custom-call | bytes 4194304 | tf_op jit(solution)/shard_map/pallas_call | solution.py:107
  6.0 0.8 %shard_map.47 = (bf16[128,512]{1,0:T(8,128)(2,1)S(1)}, bf16[128,4096]{1,0:T(8,128)(2,1)S(1)}) custom-call(bf16[64,4096]{1,0:T(8,128)(2,1)S(1)} %get-tuple-element.25.refs_0_, bf16[64,4096]{1,0:T(8,128)(2,1)S(1)} %collective-permute-done.refs_1_, bf16[4096,512]{1,0:T(8,128)(2,1)S(1)} %get-tuple-element.26.refs_2_, f32[128,128]{1,0:T(8,128)S(1)} %get-tuple-element.62.refs_3_, ...), custom_call_target="tpu_custom_call" | custom-call | flops 536870912 | bytes 4194304 | tf_op jit(solution)/shard_map/pallas_call | solution.py:123
  6.8 1.6 %collective-permute-start.2 = (bf16[128,512]{1,0:T(8,128)(2,1)S(1)}, bf16[128,512]{1,0:T(8,128)(2,1)S(1)}, u32[]{:S(2)}, u32[]{:S(2)}) collective-permute-start(bf16[128,512]{1,0:T(8,128)(2,1)S(1)} %get-tuple-element.28.refs_1_), channel_id=1, source_target_pairs={{0,8},{2,10},{4,12},{6,14},{8,16},{10,18},{12,20},{14,22},{16,24},... | collective-permute-start | bytes 393224 | tf_op jit(solution)/shard_map/ppermute | solution.py:331
  8.4 6.0 %collective-permute-done.1.refs_0_ = bf16[64,4096]{1,0:T(8,128)(2,1)S(1)} collective-permute-done((bf16[64,4096]{1,0:T(8,128)(2,1)}, bf16[64,4096]{1,0:T(8,128)(2,1)S(1)}, u32[]{:S(2)}, u32[]{:S(2)}) %collective-permute-start.1) | collective-permute-done | bytes 524320 | tf_op jit(solution)/shard_map/ppermute | solution.py:302
  14.4 0.8 %collective-permute-start.3 = (bf16[64,4096]{1,0:T(8,128)(2,1)S(1)}, bf16[64,4096]{1,0:T(8,128)(2,1)S(1)}, u32[]{:S(2)}, u32[]{:S(2)}) collective-permute-start(bf16[64,4096]{1,0:T(8,128)(2,1)S(1)} %collective-permute-done.1.refs_0_), channel_id=1, source_target_pairs={{0,2},{2,0},{4,6},{6,4},{8,10},{10,8},{12,14},{14,12},{16,18},{18,... | collective-permute-start | bytes 1572872 | tf_op jit(solution)/shard_map/ppermute | solution.py:294
  15.3 1.4 %collective-permute-done.3.refs_1_ = bf16[64,4096]{1,0:T(8,128)(2,1)S(1)} collective-permute-done((bf16[64,4096]{1,0:T(8,128)(2,1)S(1)}, bf16[64,4096]{1,0:T(8,128)(2,1)S(1)}, u32[]{:S(2)}, u32[]{:S(2)}) %collective-permute-start.3) | collective-permute-done | bytes 524320 | tf_op jit(solution)/shard_map/ppermute | solution.py:294
  16.8 0.8 %shard_map.48 = (bf16[128,512]{1,0:T(8,128)(2,1)S(1)}, bf16[128,4096]{1,0:T(8,128)(2,1)S(1)}) custom-call(bf16[64,4096]{1,0:T(8,128)(2,1)S(1)} %collective-permute-done.1.refs_0_, bf16[64,4096]{1,0:T(8,128)(2,1)S(1)} %collective-permute-done.3.refs_1_, bf16[4096,512]{1,0:T(8,128)(2,1)S(1)} %get-tuple-element.26.refs_2_, ...), custom_call_target="tpu_custom_call" | custom-call | flops 536870912 | bytes 4194304 | tf_op jit(solution)/shard_map/pallas_call | solution.py:123
  17.6 1.3 %collective-permute-start.8 = (bf16[256,512]{1,0:T(8,128)(2,1)S(1)}, bf16[256,512]{1,0:T(8,128)(2,1)S(1)}, u32[]{:S(2)}, u32[]{:S(2)}) collective-permute-start(bf16[256,512]{1,0:T(8,128)(2,1)S(1)} %get-tuple-element.59), channel_id=1, source_target_pairs={{0,8},{2,10},{4,12},{6,14},{8,16},{10,18},{12,20},{14,22},{16,24},... | collective-permute-start | bytes 786440 | tf_op jit(solution)/shard_map/ppermute | solution.py:331
  19.0 1.3 %collective-permute-start.4 = (bf16[128,512]{1,0:T(8,128)(2,1)S(1)}, bf16[128,512]{1,0:T(8,128)(2,1)S(1)}, u32[]{:S(2)}, u32[]{:S(2)}) collective-permute-start(bf16[128,512]{1,0:T(8,128)(2,1)S(1)} %get-tuple-element.31.refs_2_), channel_id=1, source_target_pairs={{0,16},{2,18},{4,20},{6,22},{8,24},{10,26},{12,28},{14,30},{1,17},... | collective-permute-start | bytes 393224 | tf_op jit(solution)/shard_map/ppermute | solution.py:331
  20.3 3.2 %collective-permute-start.5 = (bf16[384,512]{1,0:T(8,128)(2,1)S(1)}, bf16[384,512]{1,0:T(8,128)(2,1)S(1)}, u32[]{:S(2)}, u32[]{:S(2)}) collective-permute-start(bf16[384,512]{1,0:T(8,128)(2,1)S(1)} %pad_maximum_fusion), channel_id=1, source_target_pairs={{0,4},{2,6},{8,12},{10,14},{12,8},{14,10},{16,20},{18,22},{20,16},... | collective-permute-start | bytes 1179656 | tf_op jit(solution)/shard_map/ppermute | solution.py:344
  23.5 1.3 %collective-permute-start.6 = (bf16[256,512]{1,0:T(8,128)(2,1)S(1)}, bf16[256,512]{1,0:T(8,128)(2,1)S(1)}, u32[]{:S(2)}, u32[]{:S(2)}) collective-permute-start(bf16[256,512]{1,0:T(8,128)(2,1)S(1)} %get-tuple-element.60), channel_id=1, source_target_pairs={{0,24},{2,26},{4,28},{6,30},{1,25},{3,27},{5,29},{7,31}} | collective-permute-start | bytes 786440 | tf_op jit(solution)/shard_map/ppermute | solution.py:331
  24.8 3.1 %shard_map.49.refs_0_ = bf16[8,256,128]{2,1,0:T(8,128)(2,1)S(1)} custom-call(s32[11]{0:T(128)S(1)} %stack.41.facts_ref, bf16[128,4096]{1,0:T(8,128)(2,1)S(1)} %get-tuple-element.27.refs_0_, bf16[128,4096]{1,0:T(8,128)(2,1)S(1)} %get-tuple-element.30.refs_1_, bf16[4096,2048]{1,0:T(8,128)(2,1)S(1)} %copy-done, f32[256,128]{1,0:T(8,128)S(1)} %pad_maximum_fusion.5.refs_3_, ...), custom_call_target="tpu_custom_call" | custom-call | tf_op jit(solution)/shard_map/pallas_call | solution.py:141
  27.9 2.0 %shard_map.50 = (f32[8,256,128]{2,1,0:T(8,128)S(1)}, f32[8,256,128]{2,1,0:T(8,128)S(1)}, f32[8,256,128]{2,1,0:T(8,128)S(1)}) custom-call(s32[11]{0:T(128)S(1)} %stack.41.facts_ref, bf16[8,256,128]{2,1,0:T(8,128)(2,1)S(1)} %shard_map.49.refs_0_, bf16[128,512]{1,0:T(8,128)(2,1)S(1)} %get-tuple-element.28.refs_1_, ...), custom_call_target="tpu_custom_call" | custom-call | flops 402653184 | bytes 1048576 | tf_op jit(solution)/shard_map/pallas_call | solution.py:256
  30.0 2.1 %collective-permute-start.9 = (bf16[256,512]{1,0:T(8,128)(2,1)S(1)}, bf16[256,512]{1,0:T(8,128)(2,1)S(1)}, u32[]{:S(2)}, u32[]{:S(2)}) collective-permute-start(bf16[256,512]{1,0:T(8,128)(2,1)S(1)} %pad_maximum_fusion.4), channel_id=1, source_target_pairs={{8,12},{10,14},{12,8},{14,10},{16,20},{18,22},{20,16},{22,18},{24,... | collective-permute-start | bytes 786440 | tf_op jit(solution)/shard_map/ppermute | solution.py:344
  32.2 2.8 %collective-permute-done.6 = bf16[256,512]{1,0:T(8,128)(2,1)S(1)} collective-permute-done((bf16[256,512]{1,0:T(8,128)(2,1)S(1)}, bf16[256,512]{1,0:T(8,128)(2,1)S(1)}, u32[]{:S(2)}, u32[]{:S(2)}) %collective-permute-start.6) | collective-permute-done | bytes 262176 | tf_op jit(solution)/shard_map/ppermute | solution.py:331
  35.1 3.1 %collective-permute-done.4.refs_6_ = bf16[128,512]{1,0:T(8,128)(2,1)S(1)} collective-permute-done((bf16[128,512]{1,0:T(8,128)(2,1)S(1)}, bf16[128,512]{1,0:T(8,128)(2,1)S(1)}, u32[]{:S(2)}, u32[]{:S(2)}) %collective-permute-start.4) | collective-permute-done | bytes 131104 | tf_op jit(solution)/shard_map/ppermute | solution.py:331
  38.2 3.3 %collective-permute-start.7 = (bf16[384,512]{1,0:T(8,128)(2,1)S(1)}, bf16[384,512]{1,0:T(8,128)(2,1)S(1)}, u32[]{:S(2)}, u32[]{:S(2)}) collective-permute-start(bf16[384,512]{1,0:T(8,128)(2,1)S(1)} %pad_maximum_fusion.1), channel_id=1, source_target_pairs={{16,20},{18,22},{20,16},{22,18},{24,28},{26,30},{28,24},{30,26},{1... | collective-permute-start | bytes 1179656 | tf_op jit(solution)/shard_map/ppermute | solution.py:344
  41.5 5.3 %shard_map.51 = (f32[8,256,128]{2,1,0:T(8,128)S(1)}, f32[8,256,128]{2,1,0:T(8,128)S(1)}, f32[8,256,128]{2,1,0:T(8,128)S(1)}) custom-call(s32[11]{0:T(128)S(1)} %stack.41.facts_ref, bf16[8,256,128]{2,1,0:T(8,128)(2,1)S(1)} %shard_map.49.refs_0_, bf16[128,512]{1,0:T(8,128)(2,1)S(1)} %get-tuple-element.47.refs_1_, ...), custom_call_target="tpu_custom_call" | custom-call | flops 1342177280 | bytes 1048576 | tf_op jit(solution)/shard_map/pallas_call | solution.py:256
  46.9 2.6 %collective-permute-done.7 = bf16[384,512]{1,0:T(8,128)(2,1)S(1)} collective-permute-done((bf16[384,512]{1,0:T(8,128)(2,1)S(1)}, bf16[384,512]{1,0:T(8,128)(2,1)S(1)}, u32[]{:S(2)}, u32[]{:S(2)}) %collective-permute-start.7) | collective-permute-done | bytes 393248 | tf_op jit(solution)/shard_map/ppermute | solution.py:344
  49.5 2.6 %shard_map.52 = (bf16[128,1024]{1,0:T(8,128)(2,1)S(1)}, bf16[128,1024]{1,0:T(8,128)(2,1)S(1)}) custom-call(s32[11]{0:T(128)S(1)} %stack.41.facts_ref, bf16[8,256,128]{2,1,0:T(8,128)(2,1)S(1)} %shard_map.49.refs_0_, bf16[128,512]{1,0:T(8,128)(2,1)S(1)} %get-tuple-element.50.refs_1_, bf16[128,512]{1,0:T(8,128)(2,1)S(1)} %get-tuple-element.49.refs_2_, ...), custom_call_target="tpu_custom_call" | custom-call | flops 402653184 | bytes 1048576 | tf_op jit(solution)/shard_map/pallas_call | solution.py:256
  52.1 2.2 %collective-permute-start.10 = (bf16[128,1024]{1,0:T(8,128)(2,1)S(1)}, bf16[128,1024]{1,0:T(8,128)(2,1)S(1)}, u32[]{:S(2)}, u32[]{:S(2)}) collective-permute-start(bf16[128,1024]{1,0:T(8,128)(2,1)S(1)} %get-tuple-element.44), channel_id=1, source_target_pairs={{0,2},{2,0},{4,6},{6,4},{8,10},{10,8},{12,14},{14,12},{16,18},{18,... | collective-permute-start | bytes 786440 | tf_op jit(solution)/shard_map/ppermute | solution.py:294
  54.3 1.2 %collective-permute-done.10.theirs = bf16[128,1024]{1,0:T(8,128)(2,1)S(1)} collective-permute-done((bf16[128,1024]{1,0:T(8,128)(2,1)S(1)}, bf16[128,1024]{1,0:T(8,128)(2,1)S(1)}, u32[]{:S(2)}, u32[]{:S(2)}) %collective-permute-start.10) | collective-permute-done | bytes 262176 | tf_op jit(solution)/shard_map/ppermute | solution.py:294
  55.4 1.4 %shard_map.53 = bf16[128,2048]{1,0:T(8,128)(2,1)} custom-call(s32[11]{0:T(128)S(1)} %stack.41.facts_ref, bf16[128,1024]{1,0:T(8,128)(2,1)S(1)} %get-tuple-element.43.mine, bf16[128,1024]{1,0:T(8,128)(2,1)S(1)} %collective-permute-done.10.theirs), custom_call_target="tpu_custom_call" | custom-call | tf_op jit(solution)/shard_map/pallas_call | solution.py:402
  (27 shorter events, 2.0 us)
Async XLA Ops:
  0.0 6.0 %collective-permute-start = (bf16[64,4096]{1,0:T(8,128)(2,1)}, bf16[64,4096]{1,0:T(8,128)(2,1)S(1)}, u32[]{:S(2)}, u32[]{:S(2)}) collective-permute-start(bf16[64,4096]{1,0:T(8,128)(2,1)} %refs_0_.1), channel_id=1, source_target_pairs={{0,2},{2,0},{4,6},{6,4},{8,10},{10,8},{12,14},{14,12},{16,18},{18,... | collective-permute-start | bytes 1572872 | tf_op jit(solution)/shard_map/ppermute | solution.py:294
  0.7 13.8 %collective-permute-start.1 = (bf16[64,4096]{1,0:T(8,128)(2,1)}, bf16[64,4096]{1,0:T(8,128)(2,1)S(1)}, u32[]{:S(2)}, u32[]{:S(2)}) collective-permute-start(bf16[64,4096]{1,0:T(8,128)(2,1)} %refs_0_.1), channel_id=1, source_target_pairs={{0,1},{1,0},{2,3},{3,2},{4,5},{5,4},{6,7},{7,6},{8,9},{9,8},{10,11... | collective-permute-start | bytes 1572872 | tf_op jit(solution)/shard_map/ppermute | solution.py:302
  2.7 22.2 %copy-start = (bf16[4096,2048]{1,0:T(8,128)(2,1)S(1)}, bf16[4096,2048]{1,0:T(8,128)(2,1)}, u32[]{:S(2)}) copy-start(bf16[4096,2048]{1,0:T(8,128)(2,1)} %refs_2_.3) | copy-start | bytes 50331652
  6.8 7.6 %collective-permute-start.2 = (bf16[128,512]{1,0:T(8,128)(2,1)S(1)}, bf16[128,512]{1,0:T(8,128)(2,1)S(1)}, u32[]{:S(2)}, u32[]{:S(2)}) collective-permute-start(bf16[128,512]{1,0:T(8,128)(2,1)S(1)} %get-tuple-element.28.refs_1_), channel_id=1, source_target_pairs={{0,8},{2,10},{4,12},{6,14},{8,16},{10,18},{12,20},{14,22},{16,24},... | collective-permute-start | bytes 393224 | tf_op jit(solution)/shard_map/ppermute | solution.py:331
  14.4 2.3 %collective-permute-start.3 = (bf16[64,4096]{1,0:T(8,128)(2,1)S(1)}, bf16[64,4096]{1,0:T(8,128)(2,1)S(1)}, u32[]{:S(2)}, u32[]{:S(2)}) collective-permute-start(bf16[64,4096]{1,0:T(8,128)(2,1)S(1)} %collective-permute-done.1.refs_0_), channel_id=1, source_target_pairs={{0,2},{2,0},{4,6},{6,4},{8,10},{10,8},{12,14},{14,12},{16,18},{18,... | collective-permute-start | bytes 1572872 | tf_op jit(solution)/shard_map/ppermute | solution.py:294
  17.6 12.4 %collective-permute-start.8 = (bf16[256,512]{1,0:T(8,128)(2,1)S(1)}, bf16[256,512]{1,0:T(8,128)(2,1)S(1)}, u32[]{:S(2)}, u32[]{:S(2)}) collective-permute-start(bf16[256,512]{1,0:T(8,128)(2,1)S(1)} %get-tuple-element.59), channel_id=1, source_target_pairs={{0,8},{2,10},{4,12},{6,14},{8,16},{10,18},{12,20},{14,22},{16,24},... | collective-permute-start | bytes 786440 | tf_op jit(solution)/shard_map/ppermute | solution.py:331
  19.0 19.1 %collective-permute-start.4 = (bf16[128,512]{1,0:T(8,128)(2,1)S(1)}, bf16[128,512]{1,0:T(8,128)(2,1)S(1)}, u32[]{:S(2)}, u32[]{:S(2)}) collective-permute-start(bf16[128,512]{1,0:T(8,128)(2,1)S(1)} %get-tuple-element.31.refs_2_), channel_id=1, source_target_pairs={{0,16},{2,18},{4,20},{6,22},{8,24},{10,26},{12,28},{14,30},{1,17},... | collective-permute-start | bytes 393224 | tf_op jit(solution)/shard_map/ppermute | solution.py:331
  20.3 14.7 %collective-permute-start.5 = (bf16[384,512]{1,0:T(8,128)(2,1)S(1)}, bf16[384,512]{1,0:T(8,128)(2,1)S(1)}, u32[]{:S(2)}, u32[]{:S(2)}) collective-permute-start(bf16[384,512]{1,0:T(8,128)(2,1)S(1)} %pad_maximum_fusion), channel_id=1, source_target_pairs={{0,4},{2,6},{8,12},{10,14},{12,8},{14,10},{16,20},{18,22},{20,16},... | collective-permute-start | bytes 1179656 | tf_op jit(solution)/shard_map/ppermute | solution.py:344
  23.5 11.5 %collective-permute-start.6 = (bf16[256,512]{1,0:T(8,128)(2,1)S(1)}, bf16[256,512]{1,0:T(8,128)(2,1)S(1)}, u32[]{:S(2)}, u32[]{:S(2)}) collective-permute-start(bf16[256,512]{1,0:T(8,128)(2,1)S(1)} %get-tuple-element.60), channel_id=1, source_target_pairs={{0,24},{2,26},{4,28},{6,30},{1,25},{3,27},{5,29},{7,31}} | collective-permute-start | bytes 786440 | tf_op jit(solution)/shard_map/ppermute | solution.py:331
  30.0 11.5 %collective-permute-start.9 = (bf16[256,512]{1,0:T(8,128)(2,1)S(1)}, bf16[256,512]{1,0:T(8,128)(2,1)S(1)}, u32[]{:S(2)}, u32[]{:S(2)}) collective-permute-start(bf16[256,512]{1,0:T(8,128)(2,1)S(1)} %pad_maximum_fusion.4), channel_id=1, source_target_pairs={{8,12},{10,14},{12,8},{14,10},{16,20},{18,22},{20,16},{22,18},{24,... | collective-permute-start | bytes 786440 | tf_op jit(solution)/shard_map/ppermute | solution.py:344
  38.2 11.3 %collective-permute-start.7 = (bf16[384,512]{1,0:T(8,128)(2,1)S(1)}, bf16[384,512]{1,0:T(8,128)(2,1)S(1)}, u32[]{:S(2)}, u32[]{:S(2)}) collective-permute-start(bf16[384,512]{1,0:T(8,128)(2,1)S(1)} %pad_maximum_fusion.1), channel_id=1, source_target_pairs={{16,20},{18,22},{20,16},{22,18},{24,28},{26,30},{28,24},{30,26},{1... | collective-permute-start | bytes 1179656 | tf_op jit(solution)/shard_map/ppermute | solution.py:344
  52.1 3.4 %collective-permute-start.10 = (bf16[128,1024]{1,0:T(8,128)(2,1)S(1)}, bf16[128,1024]{1,0:T(8,128)(2,1)S(1)}, u32[]{:S(2)}, u32[]{:S(2)}) collective-permute-start(bf16[128,1024]{1,0:T(8,128)(2,1)S(1)} %get-tuple-element.44), channel_id=1, source_target_pairs={{0,2},{2,0},{4,6},{6,4},{8,10},{10,8},{12,14},{14,12},{16,18},{18,... | collective-permute-start | bytes 786440 | tf_op jit(solution)/shard_map/ppermute | solution.py:294
